TPU v7x, 128 devices: a whole 4x4x4 slice. The times are simulated.
128 devices in a mesh: row: 32 (over x, y, core), col: 4 (over z).
Axes of the slice: x: 4, y: 4, z: 4, core: 2. Of those that a mesh axis runs over, the one named last changes fastest.
Arguments:
- right_side: bfloat16 [65536, 4096], P(('row', 'col')), may hold values from -6 to 6
- factor: bfloat16 [65536, 2048], P(('row', 'col')), may hold values from -0.125 to 0.125
- diag_inverse: bfloat16 [2048, 512], P('col'), as said below
- tile_mask: int32 [128, 4], P(('row', 'col')), may hold values from 0 to 1, as said below
- window_rows: int32 [4], replicated, may hold values from 0 to 127, as said below
Outputs:
- solution: bfloat16 [2048, 4096], P('row', 'col')
- updated_rhs: bfloat16 [65536, 4096], P(('row', 'col'))
Inputs may be any that keep to these rules, and one draw needn't show every extreme that they name: `window_rows`: distinct stored panel numbers, panels 0 and 127 always among them; panel p is stored on device p // 1 of row+col, and the window panels lie on different devices. `tile_mask`: 0 or 1; in the row of window panel k the entries of columns k and beyond are 0. `diag_inverse`: each tile is lower triangular.
All inputs are finite; a program needn't handle non-finite values.
Results may differ from a plain program's by a relative error of at most 0.0056.
Values may be sent and summed in bfloat16 or wider, within the bound.
A program may use at most 128 MiB of HBM per device.

v0:
```python
import jax
import jax.numpy as jnp
from jax import lax
from jax.sharding import PartitionSpec as P


def spread(block, axis, source):
    block = jnp.where(lax.axis_index(axis) == source, block, jnp.zeros_like(block))
    return lax.psum(block, axis)


def tile_term(flag, tile, panel_solution):
    zeros = jnp.zeros((tile.shape[0], panel_solution.shape[1]), jnp.float32)
    return lax.cond(
        flag > 0,
        lambda: jnp.dot(tile, panel_solution, preferred_element_type=jnp.float32),
        lambda: zeros,
    )


def body(right_side, factor, diag_inverse, tile_mask, window_rows):
    panel = diag_inverse.shape[1]
    window = factor.shape[1] // panel
    pan_dev = factor.shape[0] // panel
    columns = right_side.shape[1]
    ncol = lax.axis_size("col")
    nrow = lax.axis_size("row")
    inverses = lax.all_gather(diag_inverse, "col", axis=0, tiled=True).reshape(window, panel, panel)
    col_index = lax.axis_index("col")
    row_index = lax.axis_index("row")
    accum = jnp.zeros((pan_dev * panel, columns), jnp.float32)
    solved = []
    for k in range(window):
        target = window_rows[k]
        owner = target // pan_dev
        update = accum
        residual = right_side.astype(jnp.float32) - update
        rounded = residual.astype(jnp.bfloat16)
        local_solution = jnp.dot(inverses[k], rounded, preferred_element_type=jnp.float32).astype(
            jnp.bfloat16
        )
        solution_panel = spread(local_solution, ("row", "col"), owner)
        solved.append(solution_panel)
        tile = factor[0:panel, k * panel : (k + 1) * panel]
        term = tile_term(tile_mask[0, k], tile, solution_panel)
        accum = accum.at[0:panel].add(term)
    whole = jnp.concatenate(solved, axis=0)
    updated = (right_side.astype(jnp.float32) - accum).astype(jnp.bfloat16)
    block_rows = whole.shape[0] // nrow
    block_cols = columns // ncol
    solution = lax.dynamic_slice(
        whole, (row_index * block_rows, col_index * block_cols), (block_rows, block_cols)
    )
    return (solution, updated)


def solution(mesh):
    in_specs = (
        P(("row", "col"), None),
        P(("row", "col"), None),
        P("col", None),
        P(("row", "col"), None),
        P(),
    )
    out_specs = (P("row", "col"), P(("row", "col"), None))
    return jax.shard_map(body, mesh=mesh, in_specs=in_specs, out_specs=out_specs, check_vma=False)
```

profile of v0, /device:TPU:1, one launch (start us, length us, event | category | flops | bytes accessed | tf_op | source)
XLA Modules:
  0.0 761.3 jit_solution(18041693883802960980)
XLA Ops:
  7.2 0.0 all-gather.2.cloned.1.call-start
  7.2 0.7 all-gather.2.cloned.1.call-update
  7.9 0.0 all-reduce.5.cloned.1.call-start
  8.0 1.5 fusion.30
  10.1 33.9 %all-gather.2.cloned.1.call-done = bf16[2048,512]{1,0:T(8,128)(2,1)} async-done(((bf16[512,512]{1,0:T(8,128)(2,1)}), bf16[2048,512]{1,0:T(8,128)(2,1)}) %all-gather.2.cloned.1.call-update) | async-done | bytes 2097168 | tf_op jit(solution)/shard_map/all_gather | solution.py:28
  44.0 6.7 fusion.12
  50.7 0.0 copy-start.3
  50.7 0.0 copy-start.2
  50.7 0.0 all-reduce.5.cloned.1.call-update
  50.7 0.0 all-reduce.7.cloned.1.call-start
  50.8 0.6 copy-done.3
  51.3 0.7 fusion.29
  53.3 151.5 %all-reduce.5.cloned.1.call-done = bf16[512,4096]{1,0:T(8,128)(2,1)} async-done(((bf16[512,4096]{1,0:T(8,128)(2,1)}), bf16[512,4096]{1,0:T(8,128)(2,1)}) %all-reduce.5.cloned.1.call-update) | async-done | bytes 4194320 | tf_op jit(solution)/shard_map/psum | solution.py:9
  204.8 0.0 copy-done.2
  204.8 4.3 conditional.4
  204.8 4.3 broadcast.114
  209.1 9.1 %fusion.14 = bf16[512,4096]{1,0:T(8,128)(2,1)} fusion(f32[512,4096]{1,0:T(8,128)} %get-tuple-element.134, bf16[512,4096]{1,0:T(8,128)(2,1)} %param.29, pred[]{:T(512)S(6)} %eq.13, bf16[2048,512]{1,0:T(8,128)(2,1)} %all-gather.2.cloned.1.call-done), kind=kOutput, calls=%fused_computation.26 | convolution fusion | flops 2157969408 | bytes 17301504 | tf_op jit(solution)/shard_map/dot_general | solution.py:39
  218.2 0.0 all-reduce.7.cloned.1.call-update
  218.2 0.0 all-reduce.9.cloned.1.call-start
  219.5 154.8 %all-reduce.7.cloned.1.call-done = bf16[512,4096]{1,0:T(8,128)(2,1)} async-done(((bf16[512,4096]{1,0:T(8,128)(2,1)}), bf16[512,4096]{1,0:T(8,128)(2,1)}) %all-reduce.7.cloned.1.call-update) | async-done | bytes 4194320 | tf_op jit(solution)/shard_map/psum | solution.py:9
  374.3 4.3 conditional.5
  374.3 4.3 broadcast.115
  378.6 0.0 copy-start
  378.6 11.3 %add.59 = f32[512,4096]{1,0:T(8,128)} add(f32[512,4096]{1,0:T(8,128)} %get-tuple-element.134, f32[512,4096]{1,0:T(8,128)} %get-tuple-element.135) | non-fusion elementwise | flops 2097152 | bytes 25165824 | tf_op jit(solution)/shard_map/add | solution.py:46
  389.9 0.0 copy-done
  389.9 8.1 %fusion.16 = bf16[512,4096]{1,0:T(8,128)(2,1)} fusion(f32[512,4096]{1,0:T(8,128)} %add.59, bf16[512,4096]{1,0:T(8,128)(2,1)S(1)} %copy-done, pred[]{:T(512)S(6)} %eq.14, bf16[2048,512]{1,0:T(8,128)(2,1)} %all-gather.2.cloned.1.call-done), kind=kOutput, calls=%fused_computation.28 | convolution fusion | flops 2157969408 | bytes 17301504 | tf_op jit(solution)/shard_map/dot_general | solution.py:39
  398.0 0.0 all-reduce.9.cloned.1.call-update
  398.0 0.0 all-reduce.11.cloned.1.call-start
  399.3 154.8 %all-reduce.9.cloned.1.call-done = bf16[512,4096]{1,0:T(8,128)(2,1)} async-done(((bf16[512,4096]{1,0:T(8,128)(2,1)}), bf16[512,4096]{1,0:T(8,128)(2,1)}) %all-reduce.9.cloned.1.call-update) | async-done | bytes 4194320 | tf_op jit(solution)/shard_map/psum | solution.py:9
  554.2 7.8 %conditional.6 = (f32[512,4096]{1,0:T(8,128)}) conditional(s32[]{:T(128)} %bitcast.8, () %tuple.72, (bf16[512,2048]{1,0:T(8,128)(2,1)S(1)}, bf16[512,4096]{1,0:T(8,128)(2,1)}) %tuple.103), branch_computations={%region_7.8_spmd, %region_8.9_spmd} | conditional | flops 2147483648 | bytes 13107208 | solution.py:14
  554.2 7.8 %fusion.4 = f32[512,4096]{1,0:T(8,128)} fusion(bf16[512,4096]{1,0:T(8,128)(2,1)} %get-tuple-element.121, bf16[512,2048]{1,0:T(8,128)(2,1)S(1)} %get-tuple-element.120), kind=kOutput, calls=%fused_computation.4 | convolution fusion | flops 2147483648 | bytes 13107200 | tf_op jit(solution)/shard_map/cond/branch_1_fun/dot_general | solution.py:16
  562.0 0.0 copy-start.1
  562.0 11.3 %add.60 = f32[512,4096]{1,0:T(8,128)} add(f32[512,4096]{1,0:T(8,128)} %add.59, f32[512,4096]{1,0:T(8,128)} %get-tuple-element.136) | non-fusion elementwise | flops 2097152 | bytes 25165824 | tf_op jit(solution)/shard_map/add | solution.py:46
  573.2 0.0 copy-done.1
  573.2 8.1 %fusion.18 = bf16[512,4096]{1,0:T(8,128)(2,1)} fusion(f32[512,4096]{1,0:T(8,128)} %add.60, bf16[512,4096]{1,0:T(8,128)(2,1)S(1)} %copy-done.1, pred[]{:T(512)S(6)} %eq.15, bf16[2048,512]{1,0:T(8,128)(2,1)} %all-gather.2.cloned.1.call-done), kind=kOutput, calls=%fused_computation.30 | convolution fusion | flops 2157969408 | bytes 17301504 | tf_op jit(solution)/shard_map/dot_general | solution.py:39
  581.4 0.0 all-reduce.11.cloned.1.call-update
  582.0 151.9 %all-reduce.11.cloned.1.call-done = bf16[512,4096]{1,0:T(8,128)(2,1)} async-done(((bf16[512,4096]{1,0:T(8,128)(2,1)}), bf16[512,4096]{1,0:T(8,128)(2,1)}) %all-reduce.11.cloned.1.call-update) | async-done | bytes 4194320 | tf_op jit(solution)/shard_map/psum | solution.py:9
  734.0 7.8 %conditional.7 = (f32[512,4096]{1,0:T(8,128)}) conditional(s32[]{:T(128)} %bitcast.10, () %tuple.74, (bf16[512,2048]{1,0:T(8,128)(2,1)S(1)}, bf16[512,4096]{1,0:T(8,128)(2,1)}) %tuple.104), branch_computations={%region_10.11_spmd, %region_11.12_spmd} | conditional | flops 2147483648 | bytes 13107208 | solution.py:14
  734.0 7.8 %fusion.6 = f32[512,4096]{1,0:T(8,128)} fusion(bf16[512,4096]{1,0:T(8,128)(2,1)} %get-tuple-element.123, bf16[512,2048]{1,0:T(8,128)(2,1)S(1)} %get-tuple-element.122), kind=kOutput, calls=%fused_computation.6 | convolution fusion | flops 2147483648 | bytes 13107200 | tf_op jit(solution)/shard_map/cond/branch_1_fun/dot_general | solution.py:16
  741.8 11.3 %fusion.11 = bf16[512,4096]{1,0:T(8,128)(2,1)} fusion(bf16[512,4096]{1,0:T(8,128)(2,1)} %param.29, f32[512,4096]{1,0:T(8,128)} %add.60, f32[512,4096]{1,0:T(8,128)} %get-tuple-element.137), kind=kLoop, calls=%fused_computation.19 | loop fusion | flops 8388608 | bytes 25165824 | tf_op jit(solution)/shard_map/convert_element_type | solution.py:48
  753.1 1.7 fusion.28
Async XLA Ops:
  7.2 36.8 %all-gather.2.cloned.1.call-start = ((), (), s32[]{:S(2)}) async-start(), calls=%async_computation | async-start | bytes 2621440 | tf_op jit(solution)/shard_map/all_gather | solution.py:28
  7.9 196.9 %all-reduce.5.cloned.1.call-start = ((), (), s32[]{:S(2)}) async-start(), calls=%async_computation.1 | async-start | bytes 8388608 | tf_op jit(solution)/shard_map/psum | solution.py:9
  50.7 0.7 copy-start.3
  50.7 154.1 %copy-start.2 = (bf16[512,2048]{1,0:T(8,128)(2,1)S(1)}, bf16[512,2048]{1,0:T(8,128)(2,1)}, u32[]{:S(2)}) copy-start(bf16[512,2048]{1,0:T(8,128)(2,1)} %param.30) | copy-start | bytes 6291460
  50.7 323.6 %all-reduce.7.cloned.1.call-start = ((), (), s32[]{:S(2)}) async-start(), calls=%async_computation.2 | async-start | bytes 8388608 | tf_op jit(solution)/shard_map/psum | solution.py:9
  218.2 335.9 %all-reduce.9.cloned.1.call-start = ((), (), s32[]{:S(2)}) async-start(), calls=%async_computation.3 | async-start | bytes 8388608 | tf_op jit(solution)/shard_map/psum | solution.py:9
  378.6 11.3 %copy-start = (bf16[512,4096]{1,0:T(8,128)(2,1)S(1)}, bf16[512,4096]{1,0:T(8,128)(2,1)}, u32[]{:S(2)}) copy-start(bf16[512,4096]{1,0:T(8,128)(2,1)} %param.29) | copy-start | bytes 12582916
  398.0 335.9 %all-reduce.11.cloned.1.call-start = ((), (), s32[]{:S(2)}) async-start(), calls=%async_computation.4 | async-start | bytes 8388608 | tf_op jit(solution)/shard_map/psum | solution.py:9
  562.0 11.3 %copy-start.1 = (bf16[512,4096]{1,0:T(8,128)(2,1)S(1)}, bf16[512,4096]{1,0:T(8,128)(2,1)}, u32[]{:S(2)}) copy-start(bf16[512,4096]{1,0:T(8,128)(2,1)} %param.29) | copy-start | bytes 12582916
Sparse Core Ops, SparseCore 0:
  9.7 34.2 all-gather.1
  50.8 153.9 all-reduce.4
  218.3 155.9 all-reduce.6
  398.2 155.9 all-reduce.8
  581.5 152.4 all-reduce.10
where the time goes:
time: 762 us; the launch traced here: 761 us
  waiting for transfers between devices  648 us (85%)
  matrix products  47.7 us (6%)
  other arithmetic  35.6 us (5%)
  between operations  18.9 us (2%)
  local copies, waits for them, and re-layouts  11.3 us (1%)
    psum x4, waiting for transfers between devices, spread(): return lax.psum(block, axis)  613 us
    all_gather x1, waiting for transfers between devices, body(): lax.all_gather(diag_inverse, 'col', axis=0, tiled=True)  33.9 us
    dot_general x4, matrix products, body(): jnp.dot(inverses[k], rounded, preferred_element_type=jnp.float32)  32.1 us
    add x2, other arithmetic, body(): accum = accum.at[0:panel].add(term)  22.6 us
    dot_general x2, matrix products, tile_term(): jnp.dot(tile, panel_solution, preferred_element_type=jnp.float32)  15.6 us
  transfers between devices with their start and end apart: 5, of which 5 were waited for; matrix products, arithmetic and copies ran while one was open for 0% of the time, Pallas kernels for 0%

commit v1 on v0

v1 whole, which is shorter than its diff:
```python
import jax
import jax.numpy as jnp
from jax import lax
from jax.sharding import PartitionSpec as P

AXES = ("row", "col")
NT = (((1,), (1,)), ((), ()))


def dot_nt(a, b):
    return lax.dot_general(a, b, NT, preferred_element_type=jnp.float32)


def body(right_side, factor, diag_inverse, tile_mask, window_rows):
    panel = diag_inverse.shape[1]
    window = factor.shape[1] // panel
    columns = right_side.shape[1]
    ncol = lax.axis_size("col")
    nrow = lax.axis_size("row")
    ndev = nrow * ncol
    width = columns // ndev
    col_index = lax.axis_index("col")
    row_index = lax.axis_index("row")
    me = row_index * ncol + col_index

    present = jnp.repeat(tile_mask[0] > 0, panel)
    masked = jnp.where(present[None, :], factor, jnp.zeros_like(factor))

    pieces = lax.all_to_all(
        right_side.T.reshape(ndev, width, panel), AXES, split_axis=0, concat_axis=0, tiled=True
    )

    lower = []
    for k in range(1, window):
        mine = me == window_rows[k]
        for j in range(k):
            tile = masked[:, j * panel : (j + 1) * panel]
            lower.append(jnp.where(mine, tile, jnp.zeros_like(tile)))
    lower = lax.psum(jnp.stack(lower), AXES)
    inverses = lax.all_gather(diag_inverse, "col", axis=0, tiled=True).reshape(window, panel, panel)

    solved = []
    for k in range(window):
        residual = lax.dynamic_index_in_dim(pieces, window_rows[k], 0, keepdims=False).astype(jnp.float32)
        for j in range(k):
            residual = residual - dot_nt(solved[j], lower[k * (k - 1) // 2 + j])
        solved.append(dot_nt(residual.astype(jnp.bfloat16), inverses[k]).astype(jnp.bfloat16))
    whole = lax.all_gather(jnp.concatenate(solved, axis=1), AXES, axis=0, tiled=True)

    updated = (right_side.astype(jnp.float32) - dot_nt(masked, whole)).astype(jnp.bfloat16)
    block_rows = window * panel // nrow
    block_cols = columns // ncol
    solution = lax.dynamic_slice(
        whole, (col_index * block_cols, row_index * block_rows), (block_cols, block_rows)
    ).T
    return (solution, updated)


def solution(mesh):
    in_specs = (
        P(AXES, None),
        P(AXES, None),
        P("col", None),
        P(AXES, None),
        P(),
    )
    out_specs = (P("row", "col"), P(AXES, None))
    return jax.shard_map(body, mesh=mesh, in_specs=in_specs, out_specs=out_specs, check_vma=False)
```

time: 762 us -> 339 us (0.44)
  waiting for transfers between devices: 648 us -> 260 us
  other arithmetic: 35.6 us -> 8.01 us
  matrix products: 47.7 us -> 24.5 us
  starting transfers between devices: 0.2 us -> 12.1 us
    psum x4 -> x1, waiting for transfers between devices: 613 us -> 134 us  [body(): lower = lax.psum(jnp.stack(lower), AXES)]
    all_gather x0 -> x1, waiting for transfers between devices: none -> 79.1 us  [body(): lax.all_gather(jnp.concatenate(solved, axis=1), AXES, axis=0, tiled=True)]
    dot_general x6 -> x8, matrix products: 47.7 us -> 24.5 us  [dot_nt(): return lax.dot_general(a, b, NT, preferred_element_type=jnp.float32)]
    add x2 -> x0, other arithmetic: 22.6 us -> none  [body(): accum = accum.at[0:panel].add(term)]
    all_gather x1, waiting for transfers between devices: 33.9 us -> 46.7 us  [body(): lax.all_gather(diag_inverse, 'col', axis=0, tiled=True)]
    all_to_all x0 -> x1, starting transfers between devices: none -> 12 us  [body(): lax.all_to_all(right_side.T.reshape(ndev, width, panel), AXES, split_axis...]
    convert_element_type x1 -> x0, other arithmetic: 11.3 us -> none  [body(): updated = (right_side.astype(jnp.float32) - accum).astype(jnp.bfloat16)]
    another operation x2 -> x0, local copies, waits for them, and re-layouts: 8.53 us -> none
  transfers between devices with their start and end apart: 5 -> 4, of which waited for: 5 -> 3; matrix products, arithmetic and copies ran while one was open for 0% -> 5% of each run, Pallas kernels for 0% -> 0%
where the time goes in v1:
time: 339 us
  waiting for transfers between devices  260 us (77%)
  between operations  25 us (7%)
  matrix products  24.5 us (7%)
  starting transfers between devices  12.1 us (4%)
  local copies, waits for them, and re-layouts  9 us (3%)
  other arithmetic  8.01 us (2%)
    psum x1, waiting for transfers between devices, body(): lower = lax.psum(jnp.stack(lower), AXES)  134 us
    all_gather x1, waiting for transfers between devices, body(): lax.all_gather(jnp.concatenate(solved, axis=1), AXES, axis=0, tiled=True)  79.1 us
    all_gather x1, waiting for transfers between devices, body(): lax.all_gather(diag_inverse, 'col', axis=0, tiled=True)  46.7 us
    dot_general x8, matrix products, dot_nt(): return lax.dot_general(a, b, NT, preferred_element_type=jnp.float32)  24.5 us
    all_to_all x1, starting transfers between devices, body(): lax.all_to_all(right_side.T.reshape(ndev, width, panel), AXES, split_axis...  12 us
    unnamed x8, local copies, waits for them, and re-layouts  7.29 us
  transfers between devices with their start and end apart: 4, of which 3 were waited for; matrix products, arithmetic and copies ran while one was open for 5% of the time, Pallas kernels for 0%

profile of v1, /device:TPU:1, one launch (start us, length us, event | category | flops | bytes accessed | tf_op | source)
XLA Modules:
  0.0 338.8 jit_solution(7828299529200578639)
XLA Ops:
  8.0 0.0 all-gather.3.cloned.1.call-start
  8.0 0.7 all-gather.3.cloned.1.call-update
  8.7 6.4 %copy.8 = bf16[512,4096]{0,1:T(8,128)(2,1)} copy(bf16[512,4096]{1,0:T(8,128)(2,1)} %param.5) | data formatting | bytes 8388608 | tf_op args[0]
  15.1 0.0 copy-start.1
  15.1 0.0 copy-start
  15.1 12.0 %all-to-all-start = ((bf16[128,32,512]{2,1,0:T(8,128)(2,1)}), bf16[128,32,512]{2,1,0:T(8,128)(2,1)}, u32[]{:S(2)}, u32[]{:S(2)}) async-start(bf16[128,32,512]{2,1,0:T(8,128)(2,1)} %bitcast.72), calls=%async_computation | async-start | bytes 8388608 | tf_op jit(solution)/shard_map/all_to_all | solution.py:29
  27.1 0.0 all-reduce.2.cloned.1.call-start
  27.2 0.0 copy-done.1
  27.2 0.1 broadcast_bitcast_fusion
  27.3 0.0 copy-done
  27.3 0.6 fusion.16
  29.8 1.8 broadcast_select_fusion
  31.5 0.9 bitcast_dynamic-update-slice_fusion.4
  32.5 1.0 bitcast_dynamic-update-slice_fusion.3
  33.4 0.9 bitcast_dynamic-update-slice_fusion.2
  34.3 0.9 bitcast_dynamic-update-slice_fusion.1
  35.3 0.9 bitcast_dynamic-update-slice_fusion
  36.2 0.9 fusion.7
  37.1 0.0 all-reduce.2.cloned.1.call-update
  37.1 0.0 all-gather.5.cloned.1.call-start
  44.7 46.7 %all-gather.3.cloned.1.call-done = bf16[2048,512]{1,0:T(8,128)(2,1)} async-done(((bf16[512,512]{1,0:T(8,128)(2,1)}), bf16[2048,512]{1,0:T(8,128)(2,1)}) %all-gather.3.cloned.1.call-update) | async-done | bytes 2097168 | tf_op jit(solution)/shard_map/all_gather | solution.py:40
  91.4 0.0 all-to-all-done
  91.4 1.3 convolution_convert_fusion.3
  92.7 133.6 %all-reduce.2.cloned.1.call-done = bf16[6,512,512]{2,1,0:T(8,128)(2,1)} async-done(((bf16[6,512,512]{2,1,0:T(8,128)(2,1)}), bf16[6,512,512]{2,1,0:T(8,128)(2,1)}) %all-reduce.2.cloned.1.call-update) | async-done | bytes 3145744 | tf_op jit(solution)/shard_map/psum | solution.py:39
  226.3 1.3 convolution_subtract_fusion.4
  227.6 1.6 convolution_convert_fusion.2
  229.3 1.3 convolution_subtract_fusion.2
  230.6 1.6 convolution_convert_fusion.1
  232.2 1.3 convolution_subtract_fusion.1
  233.6 1.6 convolution_convert_fusion
  235.2 0.7 pad_maximum_fusion
  235.9 0.0 all-gather.5.cloned.1.call-update
  235.9 79.1 %all-gather.5.cloned.1.call-done = bf16[4096,2048]{1,0:T(8,128)(2,1)} async-done(((bf16[32,2048]{1,0:T(8,128)(2,1)}), bf16[4096,2048]{1,0:T(8,128)(2,1)}) %all-gather.5.cloned.1.call-update) | async-done | bytes 16777232 | tf_op jit(solution)/shard_map/all_gather | solution.py:48
  315.1 1.1 dynamic-slice_bitcast_fusion
  316.2 0.8 copy.9
  317.0 14.4 %subtract_convert_fusion = bf16[512,4096]{1,0:T(8,128)(2,1)} fusion(bf16[512,4096]{1,0:T(8,128)(2,1)} %param.5, bf16[512,2048]{1,0:T(8,128)(2,1)S(1)} %broadcast_select_fusion, bf16[4096,2048]{1,0:T(8,128)(2,1)} %all-gather.5.cloned.1.call-done), kind=kOutput, calls=%fused_computation | convolution fusion | flops 8596226048 | bytes 27262976 | tf_op jit(solution)/shard_map/dot_general | solution.py:11
  (2 shorter events, 0.0 us)
Async XLA Ops:
  8.0 83.4 %all-gather.3.cloned.1.call-start = ((), (), s32[]{:S(2)}) async-start(), calls=%async_computation.1 | async-start | bytes 2621440 | tf_op jit(solution)/shard_map/all_gather | solution.py:40
  15.1 12.0 %copy-start.1 = (s32[1,4]{1,0:T(1,128)S(1)}, s32[1,4]{1,0:T(1,128)}, u32[]{:S(2)}) copy-start(s32[1,4]{1,0:T(1,128)} %param.8) | copy-start | bytes 52
  15.1 12.1 %copy-start = (s32[4]{0:T(128)S(1)}, s32[4]{0:T(128)}, u32[]{:S(2)}) copy-start(s32[4]{0:T(128)} %param.9) | copy-start | bytes 52
  15.1 76.2 %all-to-all-start = ((bf16[128,32,512]{2,1,0:T(8,128)(2,1)}), bf16[128,32,512]{2,1,0:T(8,128)(2,1)}, u32[]{:S(2)}, u32[]{:S(2)}) async-start(bf16[128,32,512]{2,1,0:T(8,128)(2,1)} %bitcast.72), calls=%async_computation | async-start | bytes 8388608 | tf_op jit(solution)/shard_map/all_to_all | solution.py:29
  27.1 199.2 %all-reduce.2.cloned.1.call-start = ((), (), s32[]{:S(2)}) async-start(), calls=%async_computation.2 | async-start | bytes 6291456 | tf_op jit(solution)/shard_map/psum | solution.py:39
  37.1 278.0 %all-gather.5.cloned.1.call-start = ((), (), s32[]{:S(2)}) async-start(), calls=%async_computation.3 | async-start | bytes 16908288 | tf_op jit(solution)/shard_map/all_gather | solution.py:48
Sparse Core Ops, SparseCore 0:
  10.6 80.7 all-gather.2
Sparse Core Ops, SparseCore 1:
  37.2 189.1 all-reduce.1
  236.0 79.0 all-gather.4

commit v2 on v1

v2 whole, which is shorter than its diff:
```python
import functools

import jax
import jax.numpy as jnp
from jax import lax
from jax.experimental import pallas as pl
from jax.experimental.pallas import tpu as pltpu
from jax.sharding import PartitionSpec as P

AXES = ("row", "col")
NT = (((1,), (1,)), ((), ()))
LANES = 128
SIDE = 4
ORDERS = ((2, 1, 0), (0, 2, 1), (1, 0, 2))


def dot_nt(a, b):
    return lax.dot_general(a, b, NT, preferred_element_type=jnp.float32)


def lane_parts(width):
    tiles = width // LANES
    sizes = [tiles // 3 + (1 if p < tiles % 3 else 0) for p in range(3)]
    starts = [sum(sizes[:p]) for p in range(3)]
    return [pl.ds(s * LANES, n * LANES) for s, n in zip(starts, sizes)]


def gather_kernel(x_ref, g_ref, local_sem, send_sem, recv_sem, side_send, side_recv):
    row, z = lax.axis_index("row"), lax.axis_index("col")
    x, y, core = row // 8, (row // 2) % 4, row % 2
    here = (x, y, z)
    parts = lane_parts(x_ref.shape[-1])

    def device(coords, c):
        return ((coords[0] * 4 + coords[1]) * 2 + c, coords[2])

    def shifted(axis, step):
        coords = list(here)
        coords[axis] = (coords[axis] + step + SIDE) % SIDE
        return coords

    partner = device(here, 1 - core)
    barrier = pltpu.get_barrier_semaphore()
    for axis in range(3):
        for step in (1, -1):
            pl.semaphore_signal(
                barrier, inc=1, device_id=device(shifted(axis, step), core),
                device_id_type=pl.DeviceIdType.MESH,
            )
    pl.semaphore_signal(barrier, inc=1, device_id=partner, device_id_type=pl.DeviceIdType.MESH)
    pl.semaphore_wait(barrier, 7)

    def block(p, f, offset, half=None):
        order = ORDERS[p]
        idx = []
        for axis in range(3):
            if axis in order[:f]:
                idx.append(pl.ds(0, SIDE))
            elif f < 3 and axis == order[f]:
                idx.append(pl.ds((here[axis] + offset + SIDE) % SIDE, 1))
            else:
                idx.append(pl.ds(here[axis], 1))
        halves = pl.ds(0, 2) if half is None else pl.ds(half, 1)
        return g_ref.at[idx[0], idx[1], pl.ds(core, 1), idx[2], halves, :, parts[p]]

    started = []

    def send(p, f, stage, way, src, dst):
        to = device(shifted(ORDERS[p][f], 1 if way == 0 else -1), core)
        copy = pltpu.make_async_remote_copy(
            src_ref=src, dst_ref=dst, send_sem=send_sem.at[p, f, stage, way],
            recv_sem=recv_sem.at[p, f, stage, way], device_id=to,
            device_id_type=pl.DeviceIdType.MESH,
        )
        copy.start()
        started.append(copy)
        return copy

    sides = []

    def hand_over(p, n, src, dst):
        copy = pltpu.make_async_remote_copy(
            src_ref=src, dst_ref=dst, send_sem=side_send.at[p, n], recv_sem=side_recv.at[p, n],
            device_id=partner, device_id_type=pl.DeviceIdType.MESH,
        )
        copy.start()
        sides.append(copy)

    first = {}
    for p in range(3):
        own = x_ref.at[:, :, :, :, :, :, parts[p]]
        first[p] = [send(p, 0, 0, way, own, block(p, 0, 0)) for way in (0, 1)]
    keep = pltpu.make_async_copy(
        x_ref, g_ref.at[pl.ds(x, 1), pl.ds(y, 1), pl.ds(core, 1), pl.ds(z, 1)], local_sem
    )
    keep.start()
    for p in range(3):
        hand_over(p, 0, x_ref.at[:, :, :, :, :, :, parts[p]], block(p, 0, 0))
    for f in range(3):
        second = {}
        for p in range(3):
            second[p] = []
            for way, offset in ((0, -1), (1, 1)):
                first[p][way].wait_recv()
                piece = block(p, f, offset, way)
                second[p].append(send(p, f, 1, way, piece, piece))
            for n, offset in ((1, -1), (2, 1)):
                whole = block(p, f, offset)
                hand_over(p, 3 * f + n, whole, whole)
        if f == 0:
            keep.wait()
        for p in range(3):
            for copy in second[p]:
                copy.wait_recv()
            if f < 2:
                own = block(p, f + 1, 0)
                first[p] = [send(p, f + 1, 0, way, own, own) for way in (0, 1)]
            far = block(p, f, 2)
            hand_over(p, 3 * f + 3, far, far)
    for copy in started:
        copy.wait_send()
    for copy in sides:
        copy.wait()


def gather_all(shard, collective_id):
    halves, rows, width = shard.shape
    return pl.pallas_call(
        gather_kernel,
        out_shape=jax.ShapeDtypeStruct((SIDE, SIDE, 2, SIDE, halves, rows, width), shard.dtype),
        in_specs=[pl.BlockSpec(memory_space=pltpu.VMEM)],
        out_specs=pl.BlockSpec(memory_space=pltpu.HBM),
        scratch_shapes=[
            pltpu.SemaphoreType.DMA,
            pltpu.SemaphoreType.DMA((3, 3, 2, 2)),
            pltpu.SemaphoreType.DMA((3, 3, 2, 2)),
            pltpu.SemaphoreType.DMA((3, 10)),
            pltpu.SemaphoreType.DMA((3, 10)),
        ],
        compiler_params=pltpu.CompilerParams(collective_id=collective_id, has_side_effects=True),
        name="gather_all_%d" % width,
    )(shard.reshape(1, 1, 1, 1, halves, rows, width))


def body(right_side, factor, diag_inverse, tile_mask, window_rows):
    panel = diag_inverse.shape[1]
    window = factor.shape[1] // panel
    columns = right_side.shape[1]
    ncol = lax.axis_size("col")
    nrow = lax.axis_size("row")
    ndev = nrow * ncol
    width = columns // ndev
    col_index = lax.axis_index("col")
    row_index = lax.axis_index("row")

    present = jnp.repeat(tile_mask[0] > 0, panel)
    masked = jnp.where(present[None, :], factor, jnp.zeros_like(factor))

    below = (window - 1) * panel
    cut = panel // nrow
    tiles = masked[:, :below].reshape(nrow, cut, ncol, below // ncol).transpose(0, 2, 1, 3)
    tiles = lax.all_to_all(
        tiles.reshape(ndev, cut, below // ncol), AXES, split_axis=0, concat_axis=0, tiled=True
    )
    pieces = lax.all_to_all(
        right_side.T.reshape(ndev, width, panel), AXES, split_axis=0, concat_axis=0, tiled=True
    )

    shard = [lax.dynamic_slice_in_dim(diag_inverse, row_index * cut, cut, 0)]
    for k in range(1, window):
        shard.append(lax.dynamic_index_in_dim(tiles, window_rows[k], 0, keepdims=False))
    shard = jnp.concatenate(shard, axis=1)
    used = shard.shape[1]
    half = -(-used // (2 * LANES)) * LANES
    shard = jnp.pad(shard, ((0, 0), (0, 2 * half - used)))
    spread = gather_all(jnp.stack([shard[:, :half], shard[:, half:]]), 0)
    spread = spread.reshape(nrow, ncol, 2, cut, half)
    spread = jnp.concatenate([spread[:, :, 0], spread[:, :, 1]], axis=3)
    inverses = spread[:, :, :, :panel].transpose(1, 0, 2, 3).reshape(window, panel, panel)
    lower = []
    for k in range(1, window):
        start = panel + (k - 1) * (below // ncol)
        part = spread[:, :, :, start : start + below // ncol]
        lower.append(part.transpose(0, 2, 1, 3).reshape(panel, below))

    solved = []
    for k in range(window):
        residual = lax.dynamic_index_in_dim(pieces, window_rows[k], 0, keepdims=False).astype(jnp.float32)
        if k > 0:
            residual = residual - dot_nt(jnp.concatenate(solved, axis=1), lower[k - 1][:, : k * panel])
        solved.append(dot_nt(residual.astype(jnp.bfloat16), inverses[k]).astype(jnp.bfloat16))
    whole = jnp.concatenate(solved, axis=1)
    whole = gather_all(whole.reshape(2, width // 2, window * panel), 1).reshape(columns, window * panel)

    updated = (right_side.astype(jnp.float32) - dot_nt(masked, whole)).astype(jnp.bfloat16)
    block_rows = window * panel // nrow
    block_cols = columns // ncol
    solution = lax.dynamic_slice(
        whole, (col_index * block_cols, row_index * block_rows), (block_cols, block_rows)
    ).T
    return (solution, updated)


def solution(mesh):
    in_specs = (
        P(AXES, None),
        P(AXES, None),
        P("col", None),
        P(AXES, None),
        P(),
    )
    out_specs = (P("row", "col"), P(AXES, None))
    return jax.shard_map(body, mesh=mesh, in_specs=in_specs, out_specs=out_specs, check_vma=False)
```

time: 339 us -> 226 us (0.67)
  waiting for transfers between devices: 260 us -> 18.5 us
  Pallas kernels: 0 us -> 123 us
  local copies, waits for them, and re-layouts: 9 us -> 32.6 us
  between operations: 25 us -> 8.35 us
  starting transfers between devices: 12.1 us -> 17 us
  other arithmetic: 8.01 us -> 3.79 us
    psum x1 -> x0, waiting for transfers between devices: 134 us -> none  [body(): lower = lax.psum(jnp.stack(lower), AXES)]
    all_gather x2 -> x0, waiting for transfers between devices: 126 us -> none  [the longest x1 79.1 us: body(): lax.all_gather(jnp.concatenate(solved, axis=1), AXES, axis=0, tiled=True)]
    pallas_call x0 -> x2, Pallas kernels: none -> 123 us  [gather_all(): pl.pallas_call(gather_kernel, out_shape=jax.ShapeDtypeStruct((SIDE, SIDE,...]
    all_to_all x0 -> x1, waiting for transfers between devices: none -> 18.5 us  [body(): lax.all_to_all(tiles.reshape(ndev, cut, below // ncol), AXES, split_axis=...]
    all_to_all x0 -> x1, starting transfers between devices: none -> 11.9 us  [body(): lax.all_to_all(tiles.reshape(ndev, cut, below // ncol), AXES, split_axis=...]
    slice x1 -> x5, local copies, waits for them, and re-layouts: 0.61 us -> 8.67 us  [the longest x1 3.78 us: body(): spread = jnp.concatenate([spread[:, :, 0], spread[:, :, 1]], axis=3)]
    all_to_all x1, starting transfers between devices: 12 us -> 5.1 us  [body(): lax.all_to_all(right_side.T.reshape(ndev, width, panel), AXES, split_axis...]
    unnamed x8 -> x15, local copies, waits for them, and re-layouts: 7.29 us -> 13.6 us
  transfers between devices with their start and end apart: 4 -> 2, of which waited for: 3 -> 1; matrix products, arithmetic and copies ran while one was open for 5% -> 10% of each run, Pallas kernels for 0% -> 32%
where the time goes in v2:
time: 226 us; the launch traced here: 225 us
  Pallas kernels  123 us (54%)
  local copies, waits for them, and re-layouts  32.6 us (14%)
  matrix products  21.6 us (10%)
  waiting for transfers between devices  18.5 us (8%)
  starting transfers between devices  17 us (8%)
  between operations  8.35 us (4%)
  other arithmetic  3.79 us (2%)
    pallas_call x2, Pallas kernels, gather_all(): pl.pallas_call(gather_kernel, out_shape=jax.ShapeDtypeStruct((SIDE, SIDE,...  123 us
    dot_general x5, matrix products, dot_nt(): return lax.dot_general(a, b, NT, preferred_element_type=jnp.float32)  21.6 us
    all_to_all x1, waiting for transfers between devices, body(): lax.all_to_all(tiles.reshape(ndev, cut, below // ncol), AXES, split_axis=...  18.5 us
    unnamed x15, local copies, waits for them, and re-layouts  13.6 us
    all_to_all x1, starting transfers between devices, body(): lax.all_to_all(tiles.reshape(ndev, cut, below // ncol), AXES, split_axis=...  11.9 us
    all_to_all x1, starting transfers between devices, body(): lax.all_to_all(right_side.T.reshape(ndev, width, panel), AXES, split_axis...  5.1 us
  transfers between devices with their start and end apart: 2, of which 1 were waited for; matrix products, arithmetic and copies ran while one was open for 10% of the time, Pallas kernels for 32%

profile of v2, /device:TPU:1, one launch (start us, length us, event | category | flops | bytes accessed | tf_op | source)
XLA Modules:
  0.0 225.1 jit_solution(4983795844334922402)
XLA Ops:
  0.6 0.0 copy-start
  0.6 0.7 compare_bitcast_fusion
  1.4 0.1 broadcast_bitcast_fusion
  1.5 1.7 broadcast_select_fusion
  3.2 1.3 slice.82
  4.5 4.0 %reshape.50 = bf16[32,16,4,384]{3,2,1,0:T(4,128)(2,1)} reshape(bf16[512,1536]{1,0:T(8,128)(2,1)} %slice.82) | data formatting | bytes 3145728 | tf_op jit(solution)/shard_map/reshape | solution.py:161
  8.4 2.9 %copy.15 = bf16[32,4,16,384]{3,2,1,0:T(8,128)(2,1)} copy(bf16[32,4,16,384]{3,1,2,0:T(4,128)(2,1)} %bitcast.93) | data formatting | bytes 3145728 | tf_op jit(solution)/shard_map/transpose | solution.py:161
  11.3 11.9 %all-to-all-start.1 = ((bf16[128,16,384]{2,1,0:T(8,128)(2,1)}), bf16[128,16,384]{2,1,0:T(8,128)(2,1)}, u32[]{:S(2)}, u32[]{:S(2)}) async-start(bf16[128,16,384]{2,1,0:T(8,128)(2,1)} %bitcast.92), calls=%async_computation.1 | async-start | bytes 3145728 | tf_op jit(solution)/shard_map/all_to_all | solution.py:162
  23.2 6.4 %copy.14 = bf16[512,4096]{0,1:T(8,128)(2,1)} copy(bf16[512,4096]{1,0:T(8,128)(2,1)} %param.5) | data formatting | bytes 8388608 | tf_op args[0]
  29.6 18.5 %all-to-all-done.1 = bf16[128,16,384]{2,1,0:T(8,128)(2,1)} async-done(((bf16[128,16,384]{2,1,0:T(8,128)(2,1)}), bf16[128,16,384]{2,1,0:T(8,128)(2,1)}, u32[]{:S(2)}, u32[]{:S(2)}) %all-to-all-start.1) | async-done | bytes 1572896 | tf_op jit(solution)/shard_map/all_to_all | solution.py:162
  48.1 0.0 copy-start.2
  48.1 5.1 %all-to-all-start = ((bf16[128,32,512]{2,1,0:T(8,128)(2,1)}), bf16[128,32,512]{2,1,0:T(8,128)(2,1)}, u32[]{:S(2)}, u32[]{:S(2)}) async-start(bf16[128,32,512]{2,1,0:T(8,128)(2,1)} %bitcast.87), calls=%async_computation | async-start | bytes 8388608 | tf_op jit(solution)/shard_map/all_to_all | solution.py:165
  53.2 0.0 copy-done.2
  53.2 0.7 fusion.53
  61.5 0.0 copy-done
  61.5 0.8 dynamic-slice_bitcast_fusion.2
  62.2 0.6 maximum_bitcast_fusion.x_ref
  62.9 71.7 %gather_all_896.1 = bf16[4,4,2,4,2,16,896]{6,5,4,3,2,1,0:T(8,128)(2,1)} custom-call(bf16[1,1,1,1,2,16,896]{6,5,4,3,2,1,0:T(8,128)(2,1)} %maximum_bitcast_fusion.x_ref), custom_call_target="tpu_custom_call" | custom-call | tf_op jit(solution)/shard_map/gather_all_896/pallas_call | solution.py:128
  134.6 3.8 %fusion.50 = (bf16[32,4,1,16,896]{4,3,2,1,0:T(8,128)(2,1)S(1)}, bf16[32,4,1,16,896]{4,3,2,1,0:T(8,128)(2,1)S(1)}) fusion(bf16[32,4,2,16,896]{4,3,2,1,0:T(8,128)(2,1)} %bitcast.84), kind=kLoop, calls=%fused_computation.61 | loop fusion | bytes 14680064 | tf_op jit(solution)/shard_map/slice | solution.py:178
  138.4 0.3 copy.30
  138.7 0.2 slice_bitcast_fusion.1
  138.9 1.2 copy.17
  140.1 1.4 copy.24
  141.5 1.8 copy.29
  143.3 1.7 fusion.51
  145.1 1.4 copy.25
  146.5 1.4 copy.26
  147.9 0.3 slice_bitcast_fusion
  148.2 1.2 fusion.52
  149.4 0.0 all-to-all-done
  149.4 1.3 convolution_convert_fusion.3
  150.7 1.7 convolution_convert_fusion.2
  152.4 1.8 convolution_convert_fusion.1
  154.2 2.2 convolution_convert_fusion
  156.4 0.7 pad_maximum_fusion
  157.1 51.5 %gather_all_2048.1 = bf16[4,4,2,4,2,16,2048]{6,5,4,3,2,1,0:T(8,128)(2,1)} custom-call(bf16[1,1,1,1,2,16,2048]{6,5,4,3,2,1,0:T(8,128)(2,1)} %bitcast.103), custom_call_target="tpu_custom_call" | custom-call | tf_op jit(solution)/shard_map/gather_all_2048/pallas_call | solution.py:128
  208.6 0.0 copy-start.1
  208.6 14.6 %subtract_convert_fusion = bf16[512,4096]{1,0:T(8,128)(2,1)} fusion(bf16[512,4096]{1,0:T(8,128)(2,1)} %param.5, bf16[512,2048]{1,0:T(8,128)(2,1)S(1)} %broadcast_select_fusion, bf16[4096,2048]{1,0:T(8,128)(2,1)} %bitcast.85), kind=kOutput, calls=%fused_computation | convolution fusion | flops 8596226048 | bytes 27262976 | tf_op jit(solution)/shard_map/dot_general | solution.py:18
  223.2 1.1 dynamic_slice.37
  224.3 0.8 copy.22
  225.1 0.0 copy-done.1
  (3 shorter events, 0.0 us)
Async XLA Ops:
  0.6 60.8 %copy-start = (bf16[512,512]{1,0:T(8,128)(2,1)S(1)}, bf16[512,512]{1,0:T(8,128)(2,1)}, u32[]{:S(2)}) copy-start(bf16[512,512]{1,0:T(8,128)(2,1)} %param.7) | copy-start | bytes 1572868
  11.3 36.8 %all-to-all-start.1 = ((bf16[128,16,384]{2,1,0:T(8,128)(2,1)}), bf16[128,16,384]{2,1,0:T(8,128)(2,1)}, u32[]{:S(2)}, u32[]{:S(2)}) async-start(bf16[128,16,384]{2,1,0:T(8,128)(2,1)} %bitcast.92), calls=%async_computation.1 | async-start | bytes 3145728 | tf_op jit(solution)/shard_map/all_to_all | solution.py:162
  48.1 5.1 %copy-start.2 = (s32[4]{0:T(128)S(1)}, s32[4]{0:T(128)}, u32[]{:S(2)}) copy-start(s32[4]{0:T(128)} %param.9) | copy-start | bytes 52
  48.1 101.3 %all-to-all-start = ((bf16[128,32,512]{2,1,0:T(8,128)(2,1)}), bf16[128,32,512]{2,1,0:T(8,128)(2,1)}, u32[]{:S(2)}, u32[]{:S(2)}) async-start(bf16[128,32,512]{2,1,0:T(8,128)(2,1)} %bitcast.87), calls=%async_computation | async-start | bytes 8388608 | tf_op jit(solution)/shard_map/all_to_all | solution.py:165
  208.6 16.5 %copy-start.1 = (bf16[512,512]{1,0:T(8,128)(2,1)S(1)}, bf16[512,512]{1,0:T(8,128)(2,1)}, u32[]{:S(2)}) copy-start(bf16[512,512]{1,0:T(8,128)(2,1)} %param.7) | copy-start | bytes 1572868

commit v3 on v2

--- a/solution.py
+++ b/solution.py
@@ -86,10 +86,19 @@
         copy.start()
         sides.append(copy)
 
+    def send_halves(p, f, halves):
+        copies = {}
+        for n in range(2):
+            for way in (0, 1):
+                half = way if n == 0 else 1 - way
+                copies[way, n] = send(p, f, n, way, halves(half), block(p, f, 0, half))
+        return copies
+
     first = {}
     for p in range(3):
-        own = x_ref.at[:, :, :, :, :, :, parts[p]]
-        first[p] = [send(p, 0, 0, way, own, block(p, 0, 0)) for way in (0, 1)]
+        first[p] = send_halves(
+            p, 0, lambda half: x_ref.at[:, :, :, :, pl.ds(half, 1), :, parts[p]]
+        )
     keep = pltpu.make_async_copy(
         x_ref, g_ref.at[pl.ds(x, 1), pl.ds(y, 1), pl.ds(core, 1), pl.ds(z, 1)], local_sem
     )
@@ -101,20 +110,21 @@
         for p in range(3):
             second[p] = []
             for way, offset in ((0, -1), (1, 1)):
-                first[p][way].wait_recv()
+                first[p][way, 0].wait_recv()
                 piece = block(p, f, offset, way)
-                second[p].append(send(p, f, 1, way, piece, piece))
-            for n, offset in ((1, -1), (2, 1)):
+                second[p].append(send(p, f, 2, way, piece, piece))
+        for p in range(3):
+            for way, offset in ((0, -1), (1, 1)):
+                first[p][way, 1].wait_recv()
                 whole = block(p, f, offset)
-                hand_over(p, 3 * f + n, whole, whole)
+                hand_over(p, 3 * f + 1 + way, whole, whole)
         if f == 0:
             keep.wait()
         for p in range(3):
             for copy in second[p]:
                 copy.wait_recv()
             if f < 2:
-                own = block(p, f + 1, 0)
-                first[p] = [send(p, f + 1, 0, way, own, own) for way in (0, 1)]
+                first[p] = send_halves(p, f + 1, lambda half: block(p, f + 1, 0, half))
             far = block(p, f, 2)
             hand_over(p, 3 * f + 3, far, far)
     for copy in started:
@@ -132,14 +142,105 @@
         out_specs=pl.BlockSpec(memory_space=pltpu.HBM),
         scratch_shapes=[
             pltpu.SemaphoreType.DMA,
-            pltpu.SemaphoreType.DMA((3, 3, 2, 2)),
-            pltpu.SemaphoreType.DMA((3, 3, 2, 2)),
+            pltpu.SemaphoreType.DMA((3, 3, 3, 2)),
+            pltpu.SemaphoreType.DMA((3, 3, 3, 2)),
             pltpu.SemaphoreType.DMA((3, 10)),
             pltpu.SemaphoreType.DMA((3, 10)),
         ],
         compiler_params=pltpu.CompilerParams(collective_id=collective_id, has_side_effects=True),
         name="gather_all_%d" % width,
     )(shard.reshape(1, 1, 1, 1, halves, rows, width))
+
+
+def cut_kernel(mask_ref, f_ref, o_ref):
+    groups, below = o_ref.shape[0], f_ref.shape[1]
+    ncol = o_ref.shape[1]
+    cut, span = o_ref.shape[2:]
+    kept = jnp.where(mask_ref[:, :below] > 0, f_ref[...], jnp.zeros_like(f_ref))
+    for g in range(groups):
+        for c in range(ncol):
+            o_ref[g, c] = kept[g * cut : (g + 1) * cut, c * span : (c + 1) * span]
+
+
+def cut_tiles(factor, present, below, nrow, ncol):
+    panel = factor.shape[0]
+    cut, span, steps = panel // nrow, below // ncol, 4
+    return pl.pallas_call(
+        cut_kernel,
+        grid=(steps,),
+        out_shape=jax.ShapeDtypeStruct((nrow, ncol, cut, span), factor.dtype),
+        in_specs=[
+            pl.BlockSpec(present.shape, lambda i: (0, 0)),
+            pl.BlockSpec((panel // steps, below), lambda i: (i, 0)),
+        ],
+        out_specs=pl.BlockSpec((nrow // steps, ncol, cut, span), lambda i: (i, 0, 0, 0)),
+        name="cut_tiles",
+    )(present, factor)
+
+
+def solve_kernel(rows_ref, pieces_ref, g_ref, o_ref, r_buf, d_buf, l_buf, r_sem, d_sem, l_sem):
+    window, _, panel = r_buf.shape
+    span = l_buf.shape[-1] // SIDE
+    right, inverse, lower = [], [], []
+    for k in range(window):
+        copy = pltpu.make_async_copy(pieces_ref.at[rows_ref[k]], r_buf.at[k], r_sem.at[k])
+        copy.start()
+        right.append(copy)
+        copy = pltpu.make_async_copy(
+            g_ref.at[:, :, :, k, 0, :, pl.ds(0, panel)], d_buf.at[k], d_sem.at[k]
+        )
+        copy.start()
+        inverse.append(copy)
+        if k == 0:
+            continue
+        half, lane = divmod(panel + (k - 1) * span, g_ref.shape[-1])
+        for z in range(SIDE):
+            copy = pltpu.make_async_copy(
+                g_ref.at[:, :, :, z, half, :, pl.ds(lane, span)],
+                l_buf.at[k - 1, :, :, :, :, pl.ds(z * span, span)],
+                l_sem.at[k - 1, z],
+            )
+            copy.start()
+            lower.append(copy)
+    for k in range(window):
+        right[k].wait()
+        residual = r_buf[k].astype(jnp.float32)
+        if k > 0:
+            for z in range(SIDE):
+                lower[(k - 1) * SIDE + z].wait()
+            tiles = l_buf[k - 1].reshape(panel, SIDE * span)
+            residual = residual - dot_nt(o_ref[:, : k * panel], tiles[:, : k * panel])
+        inverse[k].wait()
+        inv = d_buf[k].reshape(panel, panel)
+        o_ref[:, k * panel : (k + 1) * panel] = dot_nt(residual.astype(jnp.bfloat16), inv).astype(
+            jnp.bfloat16
+        )
+
+
+def solve(window_rows, pieces, spread):
+    _, width, panel = pieces.shape
+    window = window_rows.shape[0]
+    cut = spread.shape[5]
+    below = (window - 1) * panel
+    return pl.pallas_call(
+        solve_kernel,
+        out_shape=jax.ShapeDtypeStruct((width, window * panel), pieces.dtype),
+        in_specs=[
+            pl.BlockSpec(memory_space=pltpu.SMEM),
+            pl.BlockSpec(memory_space=pl.ANY),
+            pl.BlockSpec(memory_space=pl.ANY),
+        ],
+        out_specs=pl.BlockSpec(memory_space=pltpu.VMEM),
+        scratch_shapes=[
+            pltpu.VMEM((window, width, panel), pieces.dtype),
+            pltpu.VMEM((window, SIDE, SIDE, 2, cut, panel), pieces.dtype),
+            pltpu.VMEM((window - 1, SIDE, SIDE, 2, cut, below), pieces.dtype),
+            pltpu.SemaphoreType.DMA((window,)),
+            pltpu.SemaphoreType.DMA((window,)),
+            pltpu.SemaphoreType.DMA((window - 1, SIDE)),
+        ],
+        name="solve_window",
+    )(window_rows, pieces, spread)
 
 
 def body(right_side, factor, diag_inverse, tile_mask, window_rows):
@@ -158,7 +259,8 @@
 
     below = (window - 1) * panel
     cut = panel // nrow
-    tiles = masked[:, :below].reshape(nrow, cut, ncol, below // ncol).transpose(0, 2, 1, 3)
+    kept = present[None, :].astype(factor.dtype)
+    tiles = cut_tiles(factor, kept, below, nrow, ncol)
     tiles = lax.all_to_all(
         tiles.reshape(ndev, cut, below // ncol), AXES, split_axis=0, concat_axis=0, tiled=True
     )
@@ -174,22 +276,7 @@
     half = -(-used // (2 * LANES)) * LANES
     shard = jnp.pad(shard, ((0, 0), (0, 2 * half - used)))
     spread = gather_all(jnp.stack([shard[:, :half], shard[:, half:]]), 0)
-    spread = spread.reshape(nrow, ncol, 2, cut, half)
-    spread = jnp.concatenate([spread[:, :, 0], spread[:, :, 1]], axis=3)
-    inverses = spread[:, :, :, :panel].transpose(1, 0, 2, 3).reshape(window, panel, panel)
-    lower = []
-    for k in range(1, window):
-        start = panel + (k - 1) * (below // ncol)
-        part = spread[:, :, :, start : start + below // ncol]
-        lower.append(part.transpose(0, 2, 1, 3).reshape(panel, below))
-
-    solved = []
-    for k in range(window):
-        residual = lax.dynamic_index_in_dim(pieces, window_rows[k], 0, keepdims=False).astype(jnp.float32)
-        if k > 0:
-            residual = residual - dot_nt(jnp.concatenate(solved, axis=1), lower[k - 1][:, : k * panel])
-        solved.append(dot_nt(residual.astype(jnp.bfloat16), inverses[k]).astype(jnp.bfloat16))
-    whole = jnp.concatenate(solved, axis=1)
+    whole = solve(window_rows, pieces, spread)
     whole = gather_all(whole.reshape(2, width // 2, window * panel), 1).reshape(columns, window * panel)
 
     updated = (right_side.astype(jnp.float32) - dot_nt(masked, whole)).astype(jnp.bfloat16)

time: 226 us -> 200 us (0.88)
  local copies, waits for them, and re-layouts: 32.6 us -> 9.77 us
  Pallas kernels: 123 us -> 132 us
  matrix products: 21.6 us -> 14.4 us
  other arithmetic: 3.79 us -> 1.36 us
    unnamed x15 -> x11, local copies, waits for them, and re-layouts: 13.6 us -> 1.57 us
    pallas_call x0 -> x2, Pallas kernels: none -> 9.07 us  [the longest x1 5.43 us: solve(): pl.pallas_call(solve_kernel, out_shape=jax.ShapeDtypeStruct((width, windo...]
    slice x4 -> x0, local copies, waits for them, and re-layouts: 7.99 us -> none  [the longest x1 3.78 us: body(): spread = jnp.concatenate([spread[:, :, 0], spread[:, :, 1]], axis=3)]
    dot_general x5 -> x1, matrix products: 21.6 us -> 14.4 us  [dot_nt(): return lax.dot_general(a, b, NT, preferred_element_type=jnp.float32)]
    reshape x1 -> x0, local copies, waits for them, and re-layouts: 3.96 us -> none  [body(): masked[:, :below].reshape(nrow, cut, ncol, below // ncol)]
    transpose x4 -> x1, local copies, waits for them, and re-layouts: 4.5 us -> 6.41 us  [body(): right_side.T.reshape(ndev, width, panel)]
  transfers between devices with their start and end apart: 2 -> 2, of which waited for: 1 -> 1; matrix products, arithmetic and copies ran while one was open for 10% -> 4% of each run, Pallas kernels for 32% -> 36%
where the time goes in v3:
time: 200 us; the launch traced here: 199 us
  Pallas kernels  132 us (66%)
  waiting for transfers between devices  18.8 us (9%)
  starting transfers between devices  16.6 us (8%)
  matrix products  14.4 us (7%)
  local copies, waits for them, and re-layouts  9.77 us (5%)
  between operations  6.46 us (3%)
    pallas_call x2, Pallas kernels, gather_all(): pl.pallas_call(gather_kernel, out_shape=jax.ShapeDtypeStruct((SIDE, SIDE,...  123 us
    all_to_all x1, waiting for transfers between devices, body(): lax.all_to_all(tiles.reshape(ndev, cut, below // ncol), AXES, split_axis=...  18.8 us
    dot_general x1, matrix products, dot_nt(): return lax.dot_general(a, b, NT, preferred_element_type=jnp.float32)  14.4 us
    all_to_all x1, starting transfers between devices, body(): lax.all_to_all(tiles.reshape(ndev, cut, below // ncol), AXES, split_axis=...  11.5 us
    transpose x1, local copies, waits for them, and re-layouts, body(): right_side.T.reshape(ndev, width, panel)  6.41 us
    pallas_call x1, Pallas kernels, solve(): pl.pallas_call(solve_kernel, out_shape=jax.ShapeDtypeStruct((width, windo...  5.43 us
    all_to_all x1, starting transfers between devices, body(): lax.all_to_all(right_side.T.reshape(ndev, width, panel), AXES, split_axis...  5.09 us
  transfers between devices with their start and end apart: 2, of which 1 were waited for; matrix products, arithmetic and copies ran while one was open for 4% of the time, Pallas kernels for 36%

profile of v3, /device:TPU:1, one launch (start us, length us, event | category | flops | bytes accessed | tf_op | source)
XLA Modules:
  0.0 199.4 jit_solution(4686368231796286814)
XLA Ops:
  0.6 0.0 copy-start
  0.6 0.7 compare_bitcast_fusion
  1.4 0.1 broadcast_bitcast_fusion.1
  1.4 0.6 copy.10
  2.0 3.6 %cut_tiles.1 = bf16[32,4,16,384]{3,2,1,0:T(8,128)(2,1)} custom-call(bf16[1,2048]{1,0:T(2,128)(2,1)} %bitcast.40, bf16[512,2048]{1,0:T(8,128)(2,1)} %f_ref.1), custom_call_target="tpu_custom_call" | custom-call | tf_op jit(solution)/shard_map/cut_tiles/pallas_call | solution.py:168
  5.7 11.5 %all-to-all-start.1 = ((bf16[128,16,384]{2,1,0:T(8,128)(2,1)}), bf16[128,16,384]{2,1,0:T(8,128)(2,1)S(1)}, u32[]{:S(2)}, u32[]{:S(2)}) async-start(bf16[128,16,384]{2,1,0:T(8,128)(2,1)} %bitcast.36), calls=%async_computation.1 | async-start | bytes 3145728 | tf_op jit(solution)/shard_map/all_to_all | solution.py:264
  17.2 6.4 %copy.7 = bf16[4096,512]{1,0:T(8,128)(2,1)} copy(bf16[4096,512]{0,1:T(8,128)(2,1)} %bitcast.37) | data formatting | bytes 8388608 | tf_op jit(solution)/shard_map/transpose | solution.py:268
  23.6 18.8 %all-to-all-done.1 = bf16[128,16,384]{2,1,0:T(8,128)(2,1)S(1)} async-done(((bf16[128,16,384]{2,1,0:T(8,128)(2,1)}), bf16[128,16,384]{2,1,0:T(8,128)(2,1)S(1)}, u32[]{:S(2)}, u32[]{:S(2)}) %all-to-all-start.1) | async-done | bytes 1572896 | tf_op jit(solution)/shard_map/all_to_all | solution.py:264
  42.4 0.0 copy-start.2
  42.4 5.1 %all-to-all-start = ((bf16[128,32,512]{2,1,0:T(8,128)(2,1)}), bf16[128,32,512]{2,1,0:T(8,128)(2,1)}, u32[]{:S(2)}, u32[]{:S(2)}) async-start(bf16[128,32,512]{2,1,0:T(8,128)(2,1)} %bitcast.35), calls=%async_computation | async-start | bytes 8388608 | tf_op jit(solution)/shard_map/all_to_all | solution.py:267
  47.5 0.0 copy-done.2
  47.5 0.7 fusion.13
  52.0 0.1 broadcast_bitcast_fusion
  54.0 0.0 copy-done
  54.0 0.6 maximum_bitcast_fusion.x_ref
  54.7 71.8 %gather_all_896.1.g_ref = bf16[4,4,2,4,2,16,896]{6,5,4,3,2,1,0:T(8,128)(2,1)} custom-call(bf16[1,1,1,1,2,16,896]{6,5,4,3,2,1,0:T(8,128)(2,1)} %maximum_bitcast_fusion.x_ref), custom_call_target="tpu_custom_call" | custom-call | tf_op jit(solution)/shard_map/gather_all_896/pallas_call | solution.py:138
  126.5 0.0 all-to-all-done.pieces_ref
  126.5 5.4 %solve_window.1 = bf16[32,2048]{1,0:T(8,128)(2,1)} custom-call(s32[4]{0:T(128)} %rows_ref.1, bf16[128,32,512]{2,1,0:T(8,128)(2,1)} %all-to-all-done.pieces_ref, bf16[4,4,2,4,2,16,896]{6,5,4,3,2,1,0:T(8,128)(2,1)} %gather_all_896.1.g_ref), custom_call_target="tpu_custom_call" | custom-call | tf_op jit(solution)/shard_map/solve_window/pallas_call | solution.py:225
  132.0 0.0 copy-start.1
  132.0 51.1 %gather_all_2048.1 = bf16[4,4,2,4,2,16,2048]{6,5,4,3,2,1,0:T(8,128)(2,1)} custom-call(bf16[1,1,1,1,2,16,2048]{6,5,4,3,2,1,0:T(8,128)(2,1)} %bitcast.38), custom_call_target="tpu_custom_call" | custom-call | tf_op jit(solution)/shard_map/gather_all_2048/pallas_call | solution.py:138
  183.1 1.1 dynamic_slice.20
  184.2 0.8 copy.9
  185.0 0.0 copy-done.1
  185.0 14.4 %subtract_convert_fusion = bf16[512,4096]{1,0:T(8,128)(2,1)} fusion(bf16[512,4096]{1,0:T(8,128)(2,1)} %param.5, bf16[4096,2048]{1,0:T(8,128)(2,1)} %bitcast.34, bf16[512,2048]{1,0:T(8,128)(2,1)S(1)} %copy-done.1, pred[2048]{0:T(1024)(128)(4,1)S(1)} %bitcast.41), kind=kOutput, calls=%fused_computation | convolution fusion | flops 8597274624 | bytes 27265024 | tf_op jit(solution)/shard_map/dot_general | solution.py:18
  (4 shorter events, 0.0 us)
Async XLA Ops:
  0.6 53.3 %copy-start = (bf16[512,512]{1,0:T(8,128)(2,1)S(1)}, bf16[512,512]{1,0:T(8,128)(2,1)}, u32[]{:S(2)}) copy-start(bf16[512,512]{1,0:T(8,128)(2,1)} %param.7) | copy-start | bytes 1572868
  5.7 36.7 %all-to-all-start.1 = ((bf16[128,16,384]{2,1,0:T(8,128)(2,1)}), bf16[128,16,384]{2,1,0:T(8,128)(2,1)S(1)}, u32[]{:S(2)}, u32[]{:S(2)}) async-start(bf16[128,16,384]{2,1,0:T(8,128)(2,1)} %bitcast.36), calls=%async_computation.1 | async-start | bytes 3145728 | tf_op jit(solution)/shard_map/all_to_all | solution.py:264
  42.4 5.1 %copy-start.2 = (s32[4]{0:T(128)S(1)}, s32[4]{0:T(128)}, u32[]{:S(2)}) copy-start(s32[4]{0:T(128)} %rows_ref.1) | copy-start | bytes 52
  42.4 84.1 %all-to-all-start = ((bf16[128,32,512]{2,1,0:T(8,128)(2,1)}), bf16[128,32,512]{2,1,0:T(8,128)(2,1)}, u32[]{:S(2)}, u32[]{:S(2)}) async-start(bf16[128,32,512]{2,1,0:T(8,128)(2,1)} %bitcast.35), calls=%async_computation | async-start | bytes 8388608 | tf_op jit(solution)/shard_map/all_to_all | solution.py:267
  132.0 53.0 %copy-start.1 = (bf16[512,2048]{1,0:T(8,128)(2,1)S(1)}, bf16[512,2048]{1,0:T(8,128)(2,1)}, u32[]{:S(2)}) copy-start(bf16[512,2048]{1,0:T(8,128)(2,1)} %f_ref.1) | copy-start | bytes 6291460

commit v4 on v3

--- a/solution.py
+++ b/solution.py
@@ -11,6 +11,7 @@
 NT = (((1,), (1,)), ((), ()))
 LANES = 128
 SIDE = 4
+SUBS = (0, -1, 1, 2)
 ORDERS = ((2, 1, 0), (0, 2, 1), (1, 0, 2))
 
 
@@ -50,26 +51,26 @@
     pl.semaphore_signal(barrier, inc=1, device_id=partner, device_id_type=pl.DeviceIdType.MESH)
     pl.semaphore_wait(barrier, 7)
 
-    def block(p, f, offset, half=None):
+    def block(p, f, offset, half=None, sub=None):
         order = ORDERS[p]
         idx = []
         for axis in range(3):
-            if axis in order[:f]:
+            if axis == order[f]:
+                idx.append(pl.ds((here[axis] + offset + SIDE) % SIDE, 1))
+            elif axis in order[:f] and (sub is None or axis != order[f - 1]):
                 idx.append(pl.ds(0, SIDE))
-            elif f < 3 and axis == order[f]:
-                idx.append(pl.ds((here[axis] + offset + SIDE) % SIDE, 1))
             else:
-                idx.append(pl.ds(here[axis], 1))
+                idx.append(pl.ds((here[axis] + (sub or 0) + SIDE) % SIDE if axis in order[:f] else here[axis], 1))
         halves = pl.ds(0, 2) if half is None else pl.ds(half, 1)
         return g_ref.at[idx[0], idx[1], pl.ds(core, 1), idx[2], halves, :, parts[p]]
 
     started = []
 
-    def send(p, f, stage, way, src, dst):
+    def send(p, f, n, stage, way, src, dst):
         to = device(shifted(ORDERS[p][f], 1 if way == 0 else -1), core)
         copy = pltpu.make_async_remote_copy(
-            src_ref=src, dst_ref=dst, send_sem=send_sem.at[p, f, stage, way],
-            recv_sem=recv_sem.at[p, f, stage, way], device_id=to,
+            src_ref=src, dst_ref=dst, send_sem=send_sem.at[p, f, n, stage, way],
+            recv_sem=recv_sem.at[p, f, n, stage, way], device_id=to,
             device_id_type=pl.DeviceIdType.MESH,
         )
         copy.start()
@@ -86,45 +87,59 @@
         copy.start()
         sides.append(copy)
 
-    def send_halves(p, f, halves):
-        copies = {}
-        for n in range(2):
+    first = {}
+
+    def send_halves(p, f, n):
+        sub = SUBS[n] if f > 0 else None
+        for stage in range(2):
             for way in (0, 1):
-                half = way if n == 0 else 1 - way
-                copies[way, n] = send(p, f, n, way, halves(half), block(p, f, 0, half))
-        return copies
-
-    first = {}
+                half = way if stage == 0 else 1 - way
+                dst = block(p, f, 0, half, sub)
+                if f == 0 or (f == 1 and n == 0):
+                    src = x_ref.at[:, :, :, :, pl.ds(half, 1), :, parts[p]]
+                else:
+                    src = dst
+                first[p, f, n, stage, way] = send(p, f, n, stage, way, src, dst)
+
     for p in range(3):
-        first[p] = send_halves(
-            p, 0, lambda half: x_ref.at[:, :, :, :, pl.ds(half, 1), :, parts[p]]
-        )
+        send_halves(p, 0, 0)
     keep = pltpu.make_async_copy(
         x_ref, g_ref.at[pl.ds(x, 1), pl.ds(y, 1), pl.ds(core, 1), pl.ds(z, 1)], local_sem
     )
     keep.start()
     for p in range(3):
         hand_over(p, 0, x_ref.at[:, :, :, :, :, :, parts[p]], block(p, 0, 0))
+    sides_of = ((0, -1), (1, 1))
     for f in range(3):
+        if f == 1:
+            keep.wait()
+        if f < 2:
+            for p in range(3):
+                send_halves(p, f + 1, 0)
         second = {}
+        for n in range(len(SUBS) if f > 0 else 1):
+            sub = SUBS[n] if f > 0 else None
+            for p in range(3):
+                for way, offset in sides_of:
+                    first[p, f, n, 0, way].wait_recv()
+                    piece = block(p, f, offset, way, sub)
+                    second[p, n, way] = send(p, f, n, 2, way, piece, piece)
+            for p in range(3):
+                for way, offset in sides_of:
+                    first[p, f, n, 1, way].wait_recv()
         for p in range(3):
-            second[p] = []
-            for way, offset in ((0, -1), (1, 1)):
-                first[p][way, 0].wait_recv()
-                piece = block(p, f, offset, way)
-                second[p].append(send(p, f, 2, way, piece, piece))
-        for p in range(3):
-            for way, offset in ((0, -1), (1, 1)):
-                first[p][way, 1].wait_recv()
+            if f < 2:
+                send_halves(p, f + 1, 1)
+                send_halves(p, f + 1, 2)
+            for way, offset in sides_of:
                 whole = block(p, f, offset)
                 hand_over(p, 3 * f + 1 + way, whole, whole)
-        if f == 0:
-            keep.wait()
         for p in range(3):
-            for copy in second[p]:
-                copy.wait_recv()
+            for key, copy in second.items():
+                if key[0] == p:
+                    copy.wait_recv()
             if f < 2:
-                first[p] = send_halves(p, f + 1, lambda half: block(p, f + 1, 0, half))
+                send_halves(p, f + 1, 3)
             far = block(p, f, 2)
             hand_over(p, 3 * f + 3, far, far)
     for copy in started:
@@ -142,8 +157,8 @@
         out_specs=pl.BlockSpec(memory_space=pltpu.HBM),
         scratch_shapes=[
             pltpu.SemaphoreType.DMA,
-            pltpu.SemaphoreType.DMA((3, 3, 3, 2)),
-            pltpu.SemaphoreType.DMA((3, 3, 3, 2)),
+            pltpu.SemaphoreType.DMA((3, 3, 4, 3, 2)),
+            pltpu.SemaphoreType.DMA((3, 3, 4, 3, 2)),
             pltpu.SemaphoreType.DMA((3, 10)),
             pltpu.SemaphoreType.DMA((3, 10)),
         ],
@@ -152,17 +167,24 @@
     )(shard.reshape(1, 1, 1, 1, halves, rows, width))
 
 
+def keep_present(mask_ref, f_ref, count):
+    panel = f_ref.shape[1] // count
+    tiles = []
+    for j in range(count):
+        tile = f_ref[:, j * panel : (j + 1) * panel]
+        tiles.append(jnp.where(mask_ref[0, j] > 0, tile, jnp.zeros_like(tile)))
+    return jnp.concatenate(tiles, axis=1)
+
+
 def cut_kernel(mask_ref, f_ref, o_ref):
-    groups, below = o_ref.shape[0], f_ref.shape[1]
-    ncol = o_ref.shape[1]
-    cut, span = o_ref.shape[2:]
-    kept = jnp.where(mask_ref[:, :below] > 0, f_ref[...], jnp.zeros_like(f_ref))
+    groups, ncol, cut, span = o_ref.shape
+    kept = keep_present(mask_ref, f_ref, mask_ref.shape[1] - 1)
     for g in range(groups):
         for c in range(ncol):
             o_ref[g, c] = kept[g * cut : (g + 1) * cut, c * span : (c + 1) * span]
 
 
-def cut_tiles(factor, present, below, nrow, ncol):
+def cut_tiles(factor, tile_mask, below, nrow, ncol):
     panel = factor.shape[0]
     cut, span, steps = panel // nrow, below // ncol, 4
     return pl.pallas_call(
@@ -170,12 +192,12 @@
         grid=(steps,),
         out_shape=jax.ShapeDtypeStruct((nrow, ncol, cut, span), factor.dtype),
         in_specs=[
-            pl.BlockSpec(present.shape, lambda i: (0, 0)),
+            pl.BlockSpec(memory_space=pltpu.SMEM),
             pl.BlockSpec((panel // steps, below), lambda i: (i, 0)),
         ],
         out_specs=pl.BlockSpec((nrow // steps, ncol, cut, span), lambda i: (i, 0, 0, 0)),
         name="cut_tiles",
-    )(present, factor)
+    )(tile_mask, factor)
 
 
 def solve_kernel(rows_ref, pieces_ref, g_ref, o_ref, r_buf, d_buf, l_buf, r_sem, d_sem, l_sem):
@@ -243,6 +265,55 @@
     )(window_rows, pieces, spread)
 
 
+def update_kernel(place_ref, mask_ref, r_ref, f_ref, w_ref, s_ref, o_ref, kept_ref):
+    step = pl.program_id(0)
+
+    @pl.when(step == 0)
+    def _():
+        kept_ref[...] = keep_present(mask_ref, f_ref, mask_ref.shape[1])
+
+    removed = dot_nt(kept_ref[...], w_ref[...])
+    o_ref[...] = (r_ref[...].astype(jnp.float32) - removed).astype(o_ref.dtype)
+
+    @pl.when(step == place_ref[1])
+    def _():
+        rows = s_ref.shape[0]
+        per = LANES // rows
+        lane = pl.multiple_of(place_ref[0] // per * LANES, LANES)
+        tile = w_ref[:, pl.ds(lane, LANES)].astype(jnp.float32).T
+        mine = tile[:rows]
+        for n in range(1, per):
+            mine = jnp.where(place_ref[0] % per == n, tile[n * rows : (n + 1) * rows], mine)
+        s_ref[...] = mine.astype(s_ref.dtype)
+
+
+def update(place, tile_mask, right_side, factor, whole, nrow, ncol):
+    panel, columns = right_side.shape
+    step = columns // ncol
+    rows = factor.shape[1] // nrow
+    return pl.pallas_call(
+        update_kernel,
+        grid=(ncol,),
+        out_shape=(
+            jax.ShapeDtypeStruct((rows, step), whole.dtype),
+            jax.ShapeDtypeStruct(right_side.shape, right_side.dtype),
+        ),
+        in_specs=[
+            pl.BlockSpec(memory_space=pltpu.SMEM),
+            pl.BlockSpec(memory_space=pltpu.SMEM),
+            pl.BlockSpec((panel, step), lambda i: (0, i)),
+            pl.BlockSpec(factor.shape, lambda i: (0, 0), pipeline_mode=pl.Buffered(1)),
+            pl.BlockSpec((step, factor.shape[1]), lambda i: (i, 0)),
+        ],
+        out_specs=(
+            pl.BlockSpec((rows, step), lambda i: (0, 0)),
+            pl.BlockSpec((panel, step), lambda i: (0, i)),
+        ),
+        scratch_shapes=[pltpu.VMEM(factor.shape, factor.dtype)],
+        name="update_panel",
+    )(place, tile_mask, right_side, factor, whole)
+
+
 def body(right_side, factor, diag_inverse, tile_mask, window_rows):
     panel = diag_inverse.shape[1]
     window = factor.shape[1] // panel
@@ -254,13 +325,9 @@
     col_index = lax.axis_index("col")
     row_index = lax.axis_index("row")
 
-    present = jnp.repeat(tile_mask[0] > 0, panel)
-    masked = jnp.where(present[None, :], factor, jnp.zeros_like(factor))
-
     below = (window - 1) * panel
     cut = panel // nrow
-    kept = present[None, :].astype(factor.dtype)
-    tiles = cut_tiles(factor, kept, below, nrow, ncol)
+    tiles = cut_tiles(factor, tile_mask, below, nrow, ncol)
     tiles = lax.all_to_all(
         tiles.reshape(ndev, cut, below // ncol), AXES, split_axis=0, concat_axis=0, tiled=True
     )
@@ -279,12 +346,8 @@
     whole = solve(window_rows, pieces, spread)
     whole = gather_all(whole.reshape(2, width // 2, window * panel), 1).reshape(columns, window * panel)
 
-    updated = (right_side.astype(jnp.float32) - dot_nt(masked, whole)).astype(jnp.bfloat16)
-    block_rows = window * panel // nrow
-    block_cols = columns // ncol
-    solution = lax.dynamic_slice(
-        whole, (col_index * block_cols, row_index * block_rows), (block_cols, block_rows)
-    ).T
+    place = jnp.stack([row_index, col_index]).astype(jnp.int32)
+    solution, updated = update(place, tile_mask, right_side, factor, whole, nrow, ncol)
     return (solution, updated)
 
 

time: 200 us -> 193 us (0.965)
  matrix products: 14.4 us -> 0 us
  Pallas kernels: 132 us -> 142 us
  local copies, waits for them, and re-layouts: 9.77 us -> 7.09 us
    pallas_call x0 -> x1, Pallas kernels: none -> 14.7 us  [update(): pl.pallas_call(update_kernel, grid=(ncol,), out_shape=(jax.ShapeDtypeStru...]
    dot_general x1 -> x0, matrix products: 14.4 us -> none  [dot_nt(): return lax.dot_general(a, b, NT, preferred_element_type=jnp.float32)]
    pallas_call x2, Pallas kernels: 123 us -> 118 us  [gather_all(): pl.pallas_call(gather_kernel, out_shape=jax.ShapeDtypeStruct((SIDE, SIDE,...]
  transfers between devices with their start and end apart: 2 -> 2, of which waited for: 1 -> 1; matrix products, arithmetic and copies ran while one was open for 4% -> 4% of each run, Pallas kernels for 36% -> 37%
where the time goes in v4:
time: 193 us; the launch traced here: 192 us
  Pallas kernels  142 us (74%)
  waiting for transfers between devices  18.8 us (10%)
  starting transfers between devices  16.6 us (9%)
  local copies, waits for them, and re-layouts  7.09 us (4%)
  between operations  6.54 us (3%)
    pallas_call x2, Pallas kernels, gather_all(): pl.pallas_call(gather_kernel, out_shape=jax.ShapeDtypeStruct((SIDE, SIDE,...  118 us
    all_to_all x1, waiting for transfers between devices, body(): lax.all_to_all(tiles.reshape(ndev, cut, below // ncol), AXES, split_axis=...  18.8 us
    pallas_call x1, Pallas kernels, update(): pl.pallas_call(update_kernel, grid=(ncol,), out_shape=(jax.ShapeDtypeStru...  14.7 us
    all_to_all x1, starting transfers between devices, body(): lax.all_to_all(tiles.reshape(ndev, cut, below // ncol), AXES, split_axis=...  11.5 us
    transpose x1, local copies, waits for them, and re-layouts, body(): right_side.T.reshape(ndev, width, panel)  6.41 us
    pallas_call x1, Pallas kernels, solve(): pl.pallas_call(solve_kernel, out_shape=jax.ShapeDtypeStruct((width, windo...  5.43 us
    all_to_all x1, starting transfers between devices, body(): lax.all_to_all(right_side.T.reshape(ndev, width, panel), AXES, split_axis...  5.09 us
  transfers between devices with their start and end apart: 2, of which 1 were waited for; matrix products, arithmetic and copies ran while one was open for 4% of the time, Pallas kernels for 37%

profile of v4, /device:TPU:1, one launch (start us, length us, event | category | flops | bytes accessed | tf_op | source)
XLA Modules:
  0.0 192.3 jit_solution(9762851465262177418)
XLA Ops:
  0.6 0.0 copy-start
  0.6 3.7 %cut_tiles.1 = bf16[32,4,16,384]{3,2,1,0:T(8,128)(2,1)} custom-call(s32[1,4]{1,0:T(1,128)} %mask_ref.3, bf16[512,2048]{1,0:T(8,128)(2,1)} %f_ref.3), custom_call_target="tpu_custom_call" | custom-call | tf_op jit(solution)/shard_map/cut_tiles/pallas_call | solution.py:190
  4.4 11.5 %all-to-all-start.1 = ((bf16[128,16,384]{2,1,0:T(8,128)(2,1)}), bf16[128,16,384]{2,1,0:T(8,128)(2,1)S(1)}, u32[]{:S(2)}, u32[]{:S(2)}) async-start(bf16[128,16,384]{2,1,0:T(8,128)(2,1)} %bitcast.25), calls=%async_computation.1 | async-start | bytes 3145728 | tf_op jit(solution)/shard_map/all_to_all | solution.py:331
  15.9 6.4 %copy.7 = bf16[4096,512]{1,0:T(8,128)(2,1)} copy(bf16[4096,512]{0,1:T(8,128)(2,1)} %bitcast.24) | data formatting | bytes 8388608 | tf_op jit(solution)/shard_map/transpose | solution.py:335
  22.3 18.8 %all-to-all-done.1 = bf16[128,16,384]{2,1,0:T(8,128)(2,1)S(1)} async-done(((bf16[128,16,384]{2,1,0:T(8,128)(2,1)}), bf16[128,16,384]{2,1,0:T(8,128)(2,1)S(1)}, u32[]{:S(2)}, u32[]{:S(2)}) %all-to-all-start.1) | async-done | bytes 1572896 | tf_op jit(solution)/shard_map/all_to_all | solution.py:331
  41.1 0.0 copy-start.1
  41.1 5.1 %all-to-all-start = ((bf16[128,32,512]{2,1,0:T(8,128)(2,1)}), bf16[128,32,512]{2,1,0:T(8,128)(2,1)}, u32[]{:S(2)}, u32[]{:S(2)}) async-start(bf16[128,32,512]{2,1,0:T(8,128)(2,1)} %bitcast.23), calls=%async_computation | async-start | bytes 8388608 | tf_op jit(solution)/shard_map/all_to_all | solution.py:334
  46.2 0.0 copy-done.1
  46.2 0.7 fusion.8
  52.7 0.6 pad_add_fusion.place_ref
  53.3 0.0 copy-done
  53.3 0.6 maximum_bitcast_fusion.x_ref
  53.9 70.3 %gather_all_896.1.g_ref = bf16[4,4,2,4,2,16,896]{6,5,4,3,2,1,0:T(8,128)(2,1)} custom-call(bf16[1,1,1,1,2,16,896]{6,5,4,3,2,1,0:T(8,128)(2,1)} %maximum_bitcast_fusion.x_ref), custom_call_target="tpu_custom_call" | custom-call | tf_op jit(solution)/shard_map/gather_all_896/pallas_call | solution.py:153
  124.2 0.0 all-to-all-done.pieces_ref
  124.2 5.4 %solve_window.1 = bf16[32,2048]{1,0:T(8,128)(2,1)} custom-call(s32[4]{0:T(128)} %rows_ref.1, bf16[128,32,512]{2,1,0:T(8,128)(2,1)} %all-to-all-done.pieces_ref, bf16[4,4,2,4,2,16,896]{6,5,4,3,2,1,0:T(8,128)(2,1)} %gather_all_896.1.g_ref), custom_call_target="tpu_custom_call" | custom-call | tf_op jit(solution)/shard_map/solve_window/pallas_call | solution.py:247
  129.6 47.9 %gather_all_2048.1 = bf16[4,4,2,4,2,16,2048]{6,5,4,3,2,1,0:T(8,128)(2,1)} custom-call(bf16[1,1,1,1,2,16,2048]{6,5,4,3,2,1,0:T(8,128)(2,1)} %bitcast.26), custom_call_target="tpu_custom_call" | custom-call | tf_op jit(solution)/shard_map/gather_all_2048/pallas_call | solution.py:153
  177.6 14.7 %update_panel.1 = (bf16[64,1024]{1,0:T(8,128)(2,1)}, bf16[512,4096]{1,0:T(8,128)(2,1)}) custom-call(s32[2]{0:T(128)} %pad_add_fusion.place_ref, s32[1,4]{1,0:T(1,128)} %mask_ref.3, bf16[512,4096]{1,0:T(8,128)(2,1)} %r_ref.1, bf16[512,2048]{1,0:T(8,128)(2,1)} %f_ref.3, bf16[4096,2048]{1,0:T(8,128)(2,1)} %bitcast.22), custom_call_target="tpu_custom_call" | custom-call | tf_op jit(solution)/shard_map/update_panel/pallas_call | solution.py:294
  (3 shorter events, 0.0 us)
Async XLA Ops:
  0.6 52.6 %copy-start = (bf16[512,512]{1,0:T(8,128)(2,1)S(1)}, bf16[512,512]{1,0:T(8,128)(2,1)}, u32[]{:S(2)}) copy-start(bf16[512,512]{1,0:T(8,128)(2,1)} %param.7) | copy-start | bytes 1572868
  4.4 36.7 %all-to-all-start.1 = ((bf16[128,16,384]{2,1,0:T(8,128)(2,1)}), bf16[128,16,384]{2,1,0:T(8,128)(2,1)S(1)}, u32[]{:S(2)}, u32[]{:S(2)}) async-start(bf16[128,16,384]{2,1,0:T(8,128)(2,1)} %bitcast.25), calls=%async_computation.1 | async-start | bytes 3145728 | tf_op jit(solution)/shard_map/all_to_all | solution.py:331
  41.1 5.1 %copy-start.1 = (s32[4]{0:T(128)S(1)}, s32[4]{0:T(128)}, u32[]{:S(2)}) copy-start(s32[4]{0:T(128)} %rows_ref.1) | copy-start | bytes 52
  41.1 83.1 %all-to-all-start = ((bf16[128,32,512]{2,1,0:T(8,128)(2,1)}), bf16[128,32,512]{2,1,0:T(8,128)(2,1)}, u32[]{:S(2)}, u32[]{:S(2)}) async-start(bf16[128,32,512]{2,1,0:T(8,128)(2,1)} %bitcast.23), calls=%async_computation | async-start | bytes 8388608 | tf_op jit(solution)/shard_map/all_to_all | solution.py:334

commit v5 on v4

--- a/solution.py
+++ b/solution.py
@@ -178,10 +178,16 @@
 
 def cut_kernel(mask_ref, f_ref, o_ref):
     groups, ncol, cut, span = o_ref.shape
-    kept = keep_present(mask_ref, f_ref, mask_ref.shape[1] - 1)
+    count = mask_ref.shape[1] - 1
+    panel, lanes = f_ref.shape[1] // count, span // count
+    kept = keep_present(mask_ref, f_ref, count)
     for g in range(groups):
         for c in range(ncol):
-            o_ref[g, c] = kept[g * cut : (g + 1) * cut, c * span : (c + 1) * span]
+            rows = kept[g * cut : (g + 1) * cut]
+            o_ref[g, c] = jnp.concatenate(
+                [rows[:, j * panel + c * lanes : j * panel + (c + 1) * lanes] for j in range(count)],
+                axis=1,
+            )
 
 
 def cut_tiles(factor, tile_mask, below, nrow, ncol):
@@ -200,10 +206,48 @@
     )(tile_mask, factor)
 
 
+def pack_kernel(rows_ref, tiles_ref, inverse_ref, o_ref, d_buf, sem):
+    count = rows_ref.shape[0] - 1
+    _, cut, span = tiles_ref.shape
+    lanes = span // count
+    start = pl.multiple_of(lax.axis_index("row") * cut, cut)
+    copy = pltpu.make_async_copy(inverse_ref.at[pl.ds(start, cut)], d_buf, sem)
+    copy.start()
+    pieces = [tiles_ref[rows_ref[k]][:, : k * lanes] for k in range(1, count + 1)]
+    copy.wait()
+    packed = [d_buf[...]] + pieces
+    packed = jnp.concatenate(packed, axis=1)
+    half = o_ref.shape[-1]
+    o_ref[0] = packed[:, :half]
+    o_ref[1] = packed[:, half:]
+
+
+def pack(window_rows, tiles, diag_inverse):
+    _, cut, span = tiles.shape
+    count = window_rows.shape[0] - 1
+    panel = diag_inverse.shape[1]
+    width = panel + span // count * (count * (count + 1) // 2)
+    return pl.pallas_call(
+        pack_kernel,
+        out_shape=jax.ShapeDtypeStruct((2, cut, width // 2), tiles.dtype),
+        in_specs=[
+            pl.BlockSpec(memory_space=pltpu.SMEM),
+            pl.BlockSpec(memory_space=pltpu.VMEM),
+            pl.BlockSpec(memory_space=pl.ANY),
+        ],
+        out_specs=pl.BlockSpec(memory_space=pltpu.VMEM),
+        scratch_shapes=[
+            pltpu.VMEM((cut, panel), tiles.dtype),
+            pltpu.SemaphoreType.DMA,
+        ],
+        name="pack_pieces",
+    )(window_rows, tiles, diag_inverse)
+
+
 def solve_kernel(rows_ref, pieces_ref, g_ref, o_ref, r_buf, d_buf, l_buf, r_sem, d_sem, l_sem):
     window, _, panel = r_buf.shape
-    span = l_buf.shape[-1] // SIDE
-    right, inverse, lower = [], [], []
+    lanes = panel // SIDE
+    right, inverse, lower = [], [], {}
     for k in range(window):
         copy = pltpu.make_async_copy(pieces_ref.at[rows_ref[k]], r_buf.at[k], r_sem.at[k])
         copy.start()
@@ -215,23 +259,25 @@
         inverse.append(copy)
         if k == 0:
             continue
-        half, lane = divmod(panel + (k - 1) * span, g_ref.shape[-1])
-        for z in range(SIDE):
-            copy = pltpu.make_async_copy(
-                g_ref.at[:, :, :, z, half, :, pl.ds(lane, span)],
-                l_buf.at[k - 1, :, :, :, :, pl.ds(z * span, span)],
-                l_sem.at[k - 1, z],
-            )
-            copy.start()
-            lower.append(copy)
+        for j in range(k):
+            half, lane = divmod(panel + (k * (k - 1) // 2 + j) * lanes, g_ref.shape[-1])
+            for z in range(SIDE):
+                copy = pltpu.make_async_copy(
+                    g_ref.at[:, :, :, z, half, :, pl.ds(lane, lanes)],
+                    l_buf.at[k - 1, :, :, :, :, pl.ds(j * panel + z * lanes, lanes)],
+                    l_sem.at[k - 1, j, z],
+                )
+                copy.start()
+                lower[k, j, z] = copy
     for k in range(window):
         right[k].wait()
         residual = r_buf[k].astype(jnp.float32)
         if k > 0:
-            for z in range(SIDE):
-                lower[(k - 1) * SIDE + z].wait()
-            tiles = l_buf[k - 1].reshape(panel, SIDE * span)
-            residual = residual - dot_nt(o_ref[:, : k * panel], tiles[:, : k * panel])
+            for j in range(k):
+                for z in range(SIDE):
+                    lower[k, j, z].wait()
+            tiles = l_buf[k - 1, :, :, :, :, : k * panel].reshape(panel, k * panel)
+            residual = residual - dot_nt(o_ref[:, : k * panel], tiles)
         inverse[k].wait()
         inv = d_buf[k].reshape(panel, panel)
         o_ref[:, k * panel : (k + 1) * panel] = dot_nt(residual.astype(jnp.bfloat16), inv).astype(
@@ -259,7 +305,7 @@
             pltpu.VMEM((window - 1, SIDE, SIDE, 2, cut, below), pieces.dtype),
             pltpu.SemaphoreType.DMA((window,)),
             pltpu.SemaphoreType.DMA((window,)),
-            pltpu.SemaphoreType.DMA((window - 1, SIDE)),
+            pltpu.SemaphoreType.DMA((window - 1, window - 1, SIDE)),
         ],
         name="solve_window",
     )(window_rows, pieces, spread)
@@ -335,14 +381,7 @@
         right_side.T.reshape(ndev, width, panel), AXES, split_axis=0, concat_axis=0, tiled=True
     )
 
-    shard = [lax.dynamic_slice_in_dim(diag_inverse, row_index * cut, cut, 0)]
-    for k in range(1, window):
-        shard.append(lax.dynamic_index_in_dim(tiles, window_rows[k], 0, keepdims=False))
-    shard = jnp.concatenate(shard, axis=1)
-    used = shard.shape[1]
-    half = -(-used // (2 * LANES)) * LANES
-    shard = jnp.pad(shard, ((0, 0), (0, 2 * half - used)))
-    spread = gather_all(jnp.stack([shard[:, :half], shard[:, half:]]), 0)
+    spread = gather_all(pack(window_rows, tiles, diag_inverse), 0)
     whole = solve(window_rows, pieces, spread)
     whole = gather_all(whole.reshape(2, width // 2, window * panel), 1).reshape(columns, window * panel)
 

time: 193 us -> 191 us (0.990)
  between operations: 6.54 us -> 0.69 us
  Pallas kernels: 142 us -> 146 us
    pallas_call x0 -> x1, Pallas kernels: none -> 2.77 us  [pack(): pl.pallas_call(pack_kernel, out_shape=jax.ShapeDtypeStruct((2, cut, width...]
  transfers between devices with their start and end apart: 2 -> 2, of which waited for: 1 -> 1; matrix products, arithmetic and copies ran while one was open for 4% -> 4% of each run, Pallas kernels for 37% -> 39%
where the time goes in v5:
time: 191 us; the launch traced here: 190 us
  Pallas kernels  146 us (76%)
  waiting for transfers between devices  18.8 us (10%)
  starting transfers between devices  16.4 us (9%)
  local copies, waits for them, and re-layouts  7.58 us (4%)
    pallas_call x2, Pallas kernels, gather_all(): pl.pallas_call(gather_kernel, out_shape=jax.ShapeDtypeStruct((SIDE, SIDE,...  120 us
    all_to_all x1, waiting for transfers between devices, body(): lax.all_to_all(tiles.reshape(ndev, cut, below // ncol), AXES, split_axis=...  18.8 us
    pallas_call x1, Pallas kernels, update(): pl.pallas_call(update_kernel, grid=(ncol,), out_shape=(jax.ShapeDtypeStru...  14.7 us
    all_to_all x1, starting transfers between devices, body(): lax.all_to_all(tiles.reshape(ndev, cut, below // ncol), AXES, split_axis=...  11.5 us
    transpose x1, local copies, waits for them, and re-layouts, body(): right_side.T.reshape(ndev, width, panel)  6.41 us
    pallas_call x1, Pallas kernels, solve(): pl.pallas_call(solve_kernel, out_shape=jax.ShapeDtypeStruct((width, windo...  5.2 us
    all_to_all x1, starting transfers between devices, body(): lax.all_to_all(right_side.T.reshape(ndev, width, panel), AXES, split_axis...  4.95 us
  transfers between devices with their start and end apart: 2, of which 1 were waited for; matrix products, arithmetic and copies ran while one was open for 4% of the time, Pallas kernels for 39%

profile of v5, /device:TPU:1, one launch (start us, length us, event | category | flops | bytes accessed | tf_op | source)
XLA Modules:
  0.0 190.4 jit_solution(17046412572880843031)
XLA Ops:
  0.6 3.7 %cut_tiles.1 = bf16[32,4,16,384]{3,2,1,0:T(8,128)(2,1)} custom-call(s32[1,4]{1,0:T(1,128)} %mask_ref.3, bf16[512,2048]{1,0:T(8,128)(2,1)} %f_ref.3), custom_call_target="tpu_custom_call" | custom-call | tf_op jit(solution)/shard_map/cut_tiles/pallas_call | solution.py:196
  4.3 11.5 %all-to-all-start.1 = ((bf16[128,16,384]{2,1,0:T(8,128)(2,1)}), bf16[128,16,384]{2,1,0:T(8,128)(2,1)S(1)}, u32[]{:S(2)}, u32[]{:S(2)}) async-start(bf16[128,16,384]{2,1,0:T(8,128)(2,1)} %bitcast.11), calls=%async_computation.1 | async-start | bytes 3145728 | tf_op jit(solution)/shard_map/all_to_all | solution.py:377
  15.8 6.4 %copy.7 = bf16[4096,512]{1,0:T(8,128)(2,1)} copy(bf16[4096,512]{0,1:T(8,128)(2,1)} %bitcast.10) | data formatting | bytes 8388608 | tf_op jit(solution)/shard_map/transpose | solution.py:381
  22.2 18.8 %all-to-all-done.1.tiles_ref = bf16[128,16,384]{2,1,0:T(8,128)(2,1)S(1)} async-done(((bf16[128,16,384]{2,1,0:T(8,128)(2,1)}), bf16[128,16,384]{2,1,0:T(8,128)(2,1)S(1)}, u32[]{:S(2)}, u32[]{:S(2)}) %all-to-all-start.1) | async-done | bytes 1572896 | tf_op jit(solution)/shard_map/all_to_all | solution.py:377
  41.0 0.0 copy-start
  41.0 1.2 copy-done
  42.2 4.9 %all-to-all-start = ((bf16[128,32,512]{2,1,0:T(8,128)(2,1)}), bf16[128,32,512]{2,1,0:T(8,128)(2,1)}, u32[]{:S(2)}, u32[]{:S(2)}) async-start(bf16[128,32,512]{2,1,0:T(8,128)(2,1)} %bitcast.9), calls=%async_computation | async-start | bytes 8388608 | tf_op jit(solution)/shard_map/all_to_all | solution.py:380
  47.1 0.6 pad_add_fusion.place_ref
  47.8 2.8 %pack_pieces.1 = bf16[2,16,640]{2,1,0:T(8,128)(2,1)} custom-call(s32[4]{0:T(128)} %rows_ref.3, bf16[128,16,384]{2,1,0:T(8,128)(2,1)} %copy-done, bf16[512,512]{1,0:T(8,128)(2,1)} %inverse_ref.1), custom_call_target="tpu_custom_call" | custom-call | tf_op jit(solution)/shard_map/pack_pieces/pallas_call | solution.py:230
  50.5 71.9 %gather_all_640.1.g_ref = bf16[4,4,2,4,2,16,640]{6,5,4,3,2,1,0:T(8,128)(2,1)} custom-call(bf16[1,1,1,1,2,16,640]{6,5,4,3,2,1,0:T(8,128)(2,1)} %bitcast.13), custom_call_target="tpu_custom_call" | custom-call | tf_op jit(solution)/shard_map/gather_all_640/pallas_call | solution.py:153
  122.5 0.0 all-to-all-done.pieces_ref
  122.5 5.2 %solve_window.1 = bf16[32,2048]{1,0:T(8,128)(2,1)} custom-call(s32[4]{0:T(128)} %rows_ref.3, bf16[128,32,512]{2,1,0:T(8,128)(2,1)} %all-to-all-done.pieces_ref, bf16[4,4,2,4,2,16,640]{6,5,4,3,2,1,0:T(8,128)(2,1)} %gather_all_640.1.g_ref), custom_call_target="tpu_custom_call" | custom-call | tf_op jit(solution)/shard_map/solve_window/pallas_call | solution.py:293
  127.7 48.0 %gather_all_2048.1 = bf16[4,4,2,4,2,16,2048]{6,5,4,3,2,1,0:T(8,128)(2,1)} custom-call(bf16[1,1,1,1,2,16,2048]{6,5,4,3,2,1,0:T(8,128)(2,1)} %bitcast.12), custom_call_target="tpu_custom_call" | custom-call | tf_op jit(solution)/shard_map/gather_all_2048/pallas_call | solution.py:153
  175.7 14.7 %update_panel.1 = (bf16[64,1024]{1,0:T(8,128)(2,1)}, bf16[512,4096]{1,0:T(8,128)(2,1)}) custom-call(s32[2]{0:T(128)} %pad_add_fusion.place_ref, s32[1,4]{1,0:T(1,128)} %mask_ref.3, bf16[512,4096]{1,0:T(8,128)(2,1)} %r_ref.1, bf16[512,2048]{1,0:T(8,128)(2,1)} %f_ref.3, bf16[4096,2048]{1,0:T(8,128)(2,1)} %bitcast.8), custom_call_target="tpu_custom_call" | custom-call | tf_op jit(solution)/shard_map/update_panel/pallas_call | solution.py:340
Async XLA Ops:
  4.3 36.7 %all-to-all-start.1 = ((bf16[128,16,384]{2,1,0:T(8,128)(2,1)}), bf16[128,16,384]{2,1,0:T(8,128)(2,1)S(1)}, u32[]{:S(2)}, u32[]{:S(2)}) async-start(bf16[128,16,384]{2,1,0:T(8,128)(2,1)} %bitcast.11), calls=%async_computation.1 | async-start | bytes 3145728 | tf_op jit(solution)/shard_map/all_to_all | solution.py:377
  41.0 1.2 copy-start
  42.2 80.3 %all-to-all-start = ((bf16[128,32,512]{2,1,0:T(8,128)(2,1)}), bf16[128,32,512]{2,1,0:T(8,128)(2,1)}, u32[]{:S(2)}, u32[]{:S(2)}) async-start(bf16[128,32,512]{2,1,0:T(8,128)(2,1)} %bitcast.9), calls=%async_computation | async-start | bytes 8388608 | tf_op jit(solution)/shard_map/all_to_all | solution.py:380

commit v6 on v5

--- a/solution.py
+++ b/solution.py
@@ -127,6 +127,17 @@
             for p in range(3):
                 for way, offset in sides_of:
                     first[p, f, n, 1, way].wait_recv()
+                    if f == 2:
+                        piece = block(p, f, offset, None, sub)
+                        hand_over(p, 7 + 4 * way + n, piece, piece)
+        if f == 2:
+            for n in range(len(SUBS)):
+                for p in range(3):
+                    for way in (0, 1):
+                        second[p, n, way].wait_recv()
+                    piece = block(p, f, 2, None, SUBS[n])
+                    hand_over(p, 15 + n, piece, piece)
+            break
         for p in range(3):
             if f < 2:
                 send_halves(p, f + 1, 1)
@@ -159,8 +170,8 @@
             pltpu.SemaphoreType.DMA,
             pltpu.SemaphoreType.DMA((3, 3, 4, 3, 2)),
             pltpu.SemaphoreType.DMA((3, 3, 4, 3, 2)),
-            pltpu.SemaphoreType.DMA((3, 10)),
-            pltpu.SemaphoreType.DMA((3, 10)),
+            pltpu.SemaphoreType.DMA((3, 19)),
+            pltpu.SemaphoreType.DMA((3, 19)),
         ],
         compiler_params=pltpu.CompilerParams(collective_id=collective_id, has_side_effects=True),
         name="gather_all_%d" % width,

time: 191 us -> 189 us (0.990)
  transfers between devices with their start and end apart: 2 -> 2, of which waited for: 1 -> 1; matrix products, arithmetic and copies ran while one was open for 4% -> 4% of each run, Pallas kernels for 39% -> 40%
where the time goes in v6:
time: 189 us
  Pallas kernels  145 us (77%)
  waiting for transfers between devices  18.8 us (10%)
  starting transfers between devices  16.4 us (9%)
  local copies, waits for them, and re-layouts  7.58 us (4%)
    pallas_call x2, Pallas kernels, gather_all(): pl.pallas_call(gather_kernel, out_shape=jax.ShapeDtypeStruct((SIDE, SIDE,...  118 us
    all_to_all x1, waiting for transfers between devices, body(): lax.all_to_all(tiles.reshape(ndev, cut, below // ncol), AXES, split_axis=...  18.8 us
    pallas_call x1, Pallas kernels, update(): pl.pallas_call(update_kernel, grid=(ncol,), out_shape=(jax.ShapeDtypeStru...  14.7 us
    all_to_all x1, starting transfers between devices, body(): lax.all_to_all(tiles.reshape(ndev, cut, below // ncol), AXES, split_axis=...  11.5 us
    transpose x1, local copies, waits for them, and re-layouts, body(): right_side.T.reshape(ndev, width, panel)  6.41 us
    pallas_call x1, Pallas kernels, solve(): pl.pallas_call(solve_kernel, out_shape=jax.ShapeDtypeStruct((width, windo...  5.2 us
    all_to_all x1, starting transfers between devices, body(): lax.all_to_all(right_side.T.reshape(ndev, width, panel), AXES, split_axis...  4.95 us
  transfers between devices with their start and end apart: 2, of which 1 were waited for; matrix products, arithmetic and copies ran while one was open for 4% of the time, Pallas kernels for 40%

profile of v6, /device:TPU:1, one launch (start us, length us, event | category | flops | bytes accessed | tf_op | source)
XLA Modules:
  0.0 188.8 jit_solution(2906125432970549503)
XLA Ops:
  0.6 3.7 %cut_tiles.1 = bf16[32,4,16,384]{3,2,1,0:T(8,128)(2,1)} custom-call(s32[1,4]{1,0:T(1,128)} %mask_ref.3, bf16[512,2048]{1,0:T(8,128)(2,1)} %f_ref.3), custom_call_target="tpu_custom_call" | custom-call | tf_op jit(solution)/shard_map/cut_tiles/pallas_call | solution.py:207
  4.3 11.5 %all-to-all-start.1 = ((bf16[128,16,384]{2,1,0:T(8,128)(2,1)}), bf16[128,16,384]{2,1,0:T(8,128)(2,1)S(1)}, u32[]{:S(2)}, u32[]{:S(2)}) async-start(bf16[128,16,384]{2,1,0:T(8,128)(2,1)} %bitcast.11), calls=%async_computation.1 | async-start | bytes 3145728 | tf_op jit(solution)/shard_map/all_to_all | solution.py:388
  15.8 6.4 %copy.7 = bf16[4096,512]{1,0:T(8,128)(2,1)} copy(bf16[4096,512]{0,1:T(8,128)(2,1)} %bitcast.10) | data formatting | bytes 8388608 | tf_op jit(solution)/shard_map/transpose | solution.py:392
  22.2 18.8 %all-to-all-done.1.tiles_ref = bf16[128,16,384]{2,1,0:T(8,128)(2,1)S(1)} async-done(((bf16[128,16,384]{2,1,0:T(8,128)(2,1)}), bf16[128,16,384]{2,1,0:T(8,128)(2,1)S(1)}, u32[]{:S(2)}, u32[]{:S(2)}) %all-to-all-start.1) | async-done | bytes 1572896 | tf_op jit(solution)/shard_map/all_to_all | solution.py:388
  41.0 0.0 copy-start
  41.0 1.2 copy-done
  42.2 4.9 %all-to-all-start = ((bf16[128,32,512]{2,1,0:T(8,128)(2,1)}), bf16[128,32,512]{2,1,0:T(8,128)(2,1)}, u32[]{:S(2)}, u32[]{:S(2)}) async-start(bf16[128,32,512]{2,1,0:T(8,128)(2,1)} %bitcast.9), calls=%async_computation | async-start | bytes 8388608 | tf_op jit(solution)/shard_map/all_to_all | solution.py:391
  47.1 0.6 pad_add_fusion.place_ref
  47.8 2.8 %pack_pieces.1 = bf16[2,16,640]{2,1,0:T(8,128)(2,1)} custom-call(s32[4]{0:T(128)} %rows_ref.3, bf16[128,16,384]{2,1,0:T(8,128)(2,1)} %copy-done, bf16[512,512]{1,0:T(8,128)(2,1)} %inverse_ref.1), custom_call_target="tpu_custom_call" | custom-call | tf_op jit(solution)/shard_map/pack_pieces/pallas_call | solution.py:241
  50.5 72.0 %gather_all_640.1.g_ref = bf16[4,4,2,4,2,16,640]{6,5,4,3,2,1,0:T(8,128)(2,1)} custom-call(bf16[1,1,1,1,2,16,640]{6,5,4,3,2,1,0:T(8,128)(2,1)} %bitcast.13), custom_call_target="tpu_custom_call" | custom-call | tf_op jit(solution)/shard_map/gather_all_640/pallas_call | solution.py:164
  122.5 0.0 all-to-all-done.pieces_ref
  122.6 5.2 %solve_window.1 = bf16[32,2048]{1,0:T(8,128)(2,1)} custom-call(s32[4]{0:T(128)} %rows_ref.3, bf16[128,32,512]{2,1,0:T(8,128)(2,1)} %all-to-all-done.pieces_ref, bf16[4,4,2,4,2,16,640]{6,5,4,3,2,1,0:T(8,128)(2,1)} %gather_all_640.1.g_ref), custom_call_target="tpu_custom_call" | custom-call | tf_op jit(solution)/shard_map/solve_window/pallas_call | solution.py:304
  127.8 46.3 %gather_all_2048.1 = bf16[4,4,2,4,2,16,2048]{6,5,4,3,2,1,0:T(8,128)(2,1)} custom-call(bf16[1,1,1,1,2,16,2048]{6,5,4,3,2,1,0:T(8,128)(2,1)} %bitcast.12), custom_call_target="tpu_custom_call" | custom-call | tf_op jit(solution)/shard_map/gather_all_2048/pallas_call | solution.py:164
  174.1 14.7 %update_panel.1 = (bf16[64,1024]{1,0:T(8,128)(2,1)}, bf16[512,4096]{1,0:T(8,128)(2,1)}) custom-call(s32[2]{0:T(128)} %pad_add_fusion.place_ref, s32[1,4]{1,0:T(1,128)} %mask_ref.3, bf16[512,4096]{1,0:T(8,128)(2,1)} %r_ref.1, bf16[512,2048]{1,0:T(8,128)(2,1)} %f_ref.3, bf16[4096,2048]{1,0:T(8,128)(2,1)} %bitcast.8), custom_call_target="tpu_custom_call" | custom-call | tf_op jit(solution)/shard_map/update_panel/pallas_call | solution.py:351
Async XLA Ops:
  4.3 36.7 %all-to-all-start.1 = ((bf16[128,16,384]{2,1,0:T(8,128)(2,1)}), bf16[128,16,384]{2,1,0:T(8,128)(2,1)S(1)}, u32[]{:S(2)}, u32[]{:S(2)}) async-start(bf16[128,16,384]{2,1,0:T(8,128)(2,1)} %bitcast.11), calls=%async_computation.1 | async-start | bytes 3145728 | tf_op jit(solution)/shard_map/all_to_all | solution.py:388
  41.0 1.2 copy-start
  42.2 80.4 %all-to-all-start = ((bf16[128,32,512]{2,1,0:T(8,128)(2,1)}), bf16[128,32,512]{2,1,0:T(8,128)(2,1)}, u32[]{:S(2)}, u32[]{:S(2)}) async-start(bf16[128,32,512]{2,1,0:T(8,128)(2,1)} %bitcast.9), calls=%async_computation | async-start | bytes 8388608 | tf_op jit(solution)/shard_map/all_to_all | solution.py:391
